TPU v7x, 256 devices: a whole 4x4x8 slice. The times are simulated.
256 devices in a mesh: gx: 32 (over y, z), gy: 8 (over x, core).
Axes of the slice: x: 4, y: 4, z: 8, core: 2. Of those that a mesh axis runs over, the one named last changes fastest.
Arguments:
- couple_inner: float32 [32, 8, 256, 256], P('gx', 'gy'), may hold values from 0.000390625 to 0.003515625
- couple_cross: float32 [32, 8, 256, 256], P('gx', 'gy'), may hold values from 0.000390625 to 0.003515625
- couple_outer: float32 [32, 8, 256, 256], P('gx', 'gy'), may hold values from 0.000390625 to 0.003515625
- margin: float32 [32, 8, 512], P('gx', 'gy'), may hold values from 0.05 to 0.5
- sources: float32 [32, 8, 512, 128], P('gx', 'gy'), may hold values from -4 to 4
- top_values: float32 [256, 8192], P('gy', 'gx'), may hold values from -6 to 6
Outputs:
- interior_solution: float32 [32, 8, 256, 128], P('gx', 'gy')
- boundary_solution: float32 [32, 8, 256, 128], P('gx', 'gy')
All inputs are finite; a program needn't handle non-finite values.
Results may differ from a plain program's by a relative error of at most 0.0001.
Values sent between devices are 32-bit elements; how exact they have to be, the bound alone decides.
A program may use at most 128 MiB of HBM per device.

v0:
```python
import jax
import jax.numpy as jnp
import numpy as np
from jax import lax
from jax.sharding import PartitionSpec as P

LEVELS = 2


PRECISE = lax.Precision.HIGHEST
SEGMENT_TABLE = ((4, 0, 8, 2), (0, 6, 9, 3), (5, 1, 2, 10), (1, 7, 3, 11))


def swapped(x, axis, apart):
    return lax.ppermute(x, axis, [(i, i ^ 1 << apart) for i in range(lax.axis_size(axis))])


def placement_table():
    placement = np.zeros((4, 12, 4), np.float32)
    for member in range(4):
        for border in range(4):
            placement[member, SEGMENT_TABLE[member][border], border] = 1.0
    return jnp.asarray(placement, dtype=jnp.float32)


def product(left_side, right_side):
    return jnp.einsum("...ij,...jk->...ik", left_side, right_side, precision=PRECISE)


def solve_factor(factor, right_side):
    lower_solved = jax.scipy.linalg.solve_triangular(factor, right_side, lower=True)
    return jax.scipy.linalg.solve_triangular(factor, lower_solved, lower=True, trans=1)


def symmetric_part(raw_matrix):
    order_count = raw_matrix.shape[-1]
    off_diagonal = 1.0 - jnp.eye(order_count, dtype=jnp.float32)
    return 0.5 * (raw_matrix + jnp.swapaxes(raw_matrix, -1, -2)) * off_diagonal


def leaf_reduce(couple_inner, couple_cross, couple_outer, margin, sources):
    inner_couple = symmetric_part(couple_inner)
    outer_couple = symmetric_part(couple_outer)
    interior = couple_inner.shape[-1]
    border_size = couple_outer.shape[-1]
    inner_rows = jnp.sum(inner_couple, -1) + jnp.sum(couple_cross, -1)
    outer_rows = jnp.sum(outer_couple, -1) + jnp.sum(couple_cross, -2)
    inner_matrix = (
        jnp.eye(interior, dtype=jnp.float32)
        * (inner_rows * (1.0 + margin[..., :interior]))[..., None]
        - inner_couple
    )
    outer_matrix = (
        jnp.eye(border_size, dtype=jnp.float32)
        * (outer_rows * (1.0 + margin[..., interior:]))[..., None]
        - outer_couple
    )
    cross_matrix = -couple_cross
    factor = jnp.linalg.cholesky(inner_matrix)
    solved = solve_factor(factor, jnp.concatenate([cross_matrix, sources[..., :interior, :]], -1))
    reduced = product(jnp.swapaxes(cross_matrix, -1, -2), solved)
    boundary_map = outer_matrix - reduced[..., :border_size]
    boundary_flux = sources[..., interior:, :] - reduced[..., border_size:]
    return (boundary_map, boundary_flux, solved)


def assemble(child_maps, child_fluxes):
    placement = placement_table()
    length = child_maps.shape[-1] // 4
    blocks = child_maps.reshape(child_maps.shape[:-2] + (4, length, 4, length))
    assembled = jnp.einsum(
        "cps,c...sltm,cqt->...plqm", placement, blocks, placement, precision=PRECISE
    )
    assembled = assembled.reshape(assembled.shape[:-4] + (12 * length, 12 * length))
    flux_blocks = child_fluxes.reshape(
        child_fluxes.shape[:-2] + (4, length, child_fluxes.shape[-1])
    )
    assembled_flux = jnp.einsum("cps,c...slm->...plm", placement, flux_blocks, precision=PRECISE)
    assembled_flux = assembled_flux.reshape(
        assembled_flux.shape[:-3] + (12 * length, child_fluxes.shape[-1])
    )
    return (assembled, assembled_flux)


def merge_level(assembled, assembled_flux):
    inside = assembled.shape[-1] // 3
    outer_size = assembled.shape[-1] - inside
    factor = jnp.linalg.cholesky(assembled[..., :inside, :inside])
    solved = solve_factor(
        factor,
        jnp.concatenate([assembled[..., :inside, inside:], assembled_flux[..., :inside, :]], -1),
    )
    reduced = product(assembled[..., inside:, :inside], solved)
    parent_map = assembled[..., inside:, inside:] - reduced[..., :outer_size]
    parent_flux = assembled_flux[..., inside:, :] - reduced[..., outer_size:]
    return (parent_map, parent_flux, solved)


def child_values(full_values, length):
    placement = placement_table()
    blocks = full_values.reshape(full_values.shape[:-2] + (12, length, full_values.shape[-1]))
    picked = jnp.einsum("cps,...plm->c...slm", placement, blocks, precision=PRECISE)
    return picked.reshape(picked.shape[:-3] + (4 * length, full_values.shape[-1]))


def choose_by(selector, when_set, otherwise):
    return tuple(
        (jnp.where(selector == 1, first, second) for first, second in zip(when_set, otherwise))
    )


def gather_children(carried, level_index, bit_column, bit_row):
    partner = swapped((carried[0], carried[1], carried[2]), "gx", level_index)
    left_half = choose_by(bit_column, partner, carried)
    right_half = choose_by(bit_column, carried, partner)
    row_pair = (
        jnp.stack([left_half[0], right_half[0]]),
        jnp.stack([left_half[1], right_half[1]]),
        jnp.concatenate([left_half[2], right_half[2]], 1),
    )
    partner_pair = swapped((row_pair[0], row_pair[1], row_pair[2]), "gy", level_index)
    lower_pair = choose_by(bit_row, partner_pair, row_pair)
    upper_pair = choose_by(bit_row, row_pair, partner_pair)
    child_maps = jnp.stack([lower_pair[0][0], lower_pair[0][1], upper_pair[0][0], upper_pair[0][1]])
    child_fluxes = jnp.stack(
        [lower_pair[1][0], lower_pair[1][1], upper_pair[1][0], upper_pair[1][1]]
    )
    pieces = jnp.concatenate([lower_pair[2], upper_pair[2]], 0)
    return (child_maps, child_fluxes, pieces)


def deliver(offspring, bit_column, bit_row):
    layout = offspring.reshape((2, 2) + offspring.shape[1:])
    row_pick = lax.dynamic_index_in_dim(layout, bit_row, 0, keepdims=False)
    return lax.dynamic_index_in_dim(row_pick, bit_column, 0, keepdims=False)


def local(couple_inner, couple_cross, couple_outer, margin, sources, top_values):
    boundary_map, boundary_flux, leaf_solved = leaf_reduce(
        couple_inner[0, 0], couple_cross[0, 0], couple_outer[0, 0], margin[0, 0], sources[0, 0]
    )
    carried = (boundary_map, boundary_flux, top_values)
    saved = []
    for level_index in range(LEVELS):
        spacing = 2**level_index
        bit_column = lax.axis_index("gx") // spacing % 2
        bit_row = lax.axis_index("gy") // spacing % 2
        child_maps, child_fluxes, pieces = gather_children(
            carried, level_index, bit_column, bit_row
        )
        assembled, assembled_flux = assemble(child_maps, child_fluxes)
        if level_index + 1 < LEVELS:
            parent_map, parent_flux, solved = merge_level(assembled, assembled_flux)
            saved.append((solved, bit_column, bit_row))
            carried = (parent_map, parent_flux, pieces)
    inside = assembled.shape[-1] // 3
    top_data = pieces.T
    factor = jnp.linalg.cholesky(assembled[:inside, :inside])
    right_side = assembled_flux[:inside, :] - product(assembled[:inside, inside:], top_data)
    inner_values = solve_factor(factor, right_side)
    values = deliver(
        child_values(jnp.concatenate([inner_values, top_data], 0), inside // 4), bit_column, bit_row
    )
    for solved, bit_column, bit_row in reversed(saved):
        outer_size = solved.shape[-1] - values.shape[-1]
        inner_values = solved[:, outer_size:] - product(solved[:, :outer_size], values)
        values = deliver(
            child_values(jnp.concatenate([inner_values, values], 0), solved.shape[0] // 4),
            bit_column,
            bit_row,
        )
    border_size = values.shape[0]
    interior_solution = leaf_solved[:, border_size:] - product(leaf_solved[:, :border_size], values)
    return (interior_solution[None, None], values[None, None])


def solution(mesh):
    return jax.shard_map(
        local,
        mesh=mesh,
        in_specs=(
            P("gx", "gy", None, None),
            P("gx", "gy", None, None),
            P("gx", "gy", None, None),
            P("gx", "gy", None),
            P("gx", "gy", None, None),
            P("gy", "gx"),
        ),
        out_specs=(P("gx", "gy", None, None), P("gx", "gy", None, None)),
        check_vma=False,
    )
```

profile of v0, /device:TPU:1, one launch (start us, length us, event | category | flops | bytes accessed | tf_op | source)
XLA Modules:
  0.0 572.1 jit_solution(879543722312901472)
XLA Ops:
  9.1 11.7 %cholesky.357 = f32[128,128]{1,0:T(8,128)S(1)} custom-call(f32[128,128]{1,0:T(8,128)S(1)} %copy.67), custom_call_target="Cholesky" | custom-call | tf_op jit(solution)/shard_map/jit(cholesky)/cholesky | solution.py:59
  20.9 9.8 %custom-call.59 = f32[1,128,128]{1,2,0:T(8,128)S(1)} custom-call(f32[1,128,128]{2,1,0:T(8,128)S(1)} %get-tuple-element.102), custom_call_target="InvertDiagBlocksLowerTriangular" | custom-call | tf_op jit(solution)/shard_map/jit(cholesky)/cholesky/custom-call.12 | solution.py:59
  31.4 11.7 %cholesky.367 = f32[128,128]{1,0:T(8,128)S(1)} custom-call(f32[128,128]{1,0:T(8,128)S(1)} %copy.70), custom_call_target="Cholesky" | custom-call | tf_op jit(solution)/shard_map/jit(cholesky)/cholesky | solution.py:59
  45.9 4.2 while.3
  50.6 19.7 %custom-call.50 = f32[2,128,128]{1,2,0:T(8,128)S(1)} custom-call(f32[2,128,128]{2,1,0:T(8,128)S(1)} %get-tuple-element.11), custom_call_target="InvertDiagBlocksLowerTriangular" | custom-call | tf_op jit(solution)/shard_map/jit(_solve_triangular)/triangular_solve | solution.py:32
  73.1 2.5 collective-permute-start.2
  78.0 4.8 collective-permute-start.3
  83.5 2.6 collective-permute-start.1
  89.2 2.5 reshape.152
  91.8 8.2 %fusion.14 = f32[4,64,4,64,12]{3,4,2,1,0:T(8,128)S(1)} fusion(f32[4,12,4,1,1]{1,2,4,3,0:T(4,128)S(1)} %copy-done.23, f32[4,4,64,4,64]{4,3,2,1,0:T(4,128)S(1)} %reshape.152), kind=kOutput, calls=%fused_computation.19 | convolution fusion | flops 37748736 | bytes 4195072 | tf_op jit(solution)/shard_map/cps,c...sltm,cqt->...plqm/dot_general | solution.py:71
  100.1 11.4 %fusion.9 = f32[12,64,12,64]{3,2,0,1:T(8,128)S(1)} fusion(f32[4,12,4,1,1]{1,2,0,4,3:T(4,128)S(1)} %copy-done.22, f32[4,64,4,64,12]{3,4,2,1,0:T(8,128)S(1)} %fusion.14), kind=kOutput, calls=%fused_computation.15 | convolution fusion | flops 113246208 | bytes 5505792 | tf_op jit(solution)/shard_map/cps,c...sltm,cqt->...plqm/dot_general | solution.py:71
  111.4 3.2 copy.75
  114.6 4.2 reshape.153
  123.1 11.7 %cholesky.384 = f32[128,128]{1,0:T(8,128)S(1)} custom-call(f32[128,128]{1,0:T(8,128)S(1)} %cholesky.410), custom_call_target="Cholesky" | custom-call | tf_op jit(solution)/shard_map/jit(cholesky)/cholesky | solution.py:88
  136.1 9.8 %custom-call.60 = f32[1,128,128]{1,2,0:T(8,128)S(1)} custom-call(f32[1,128,128]{2,1,0:T(8,128)S(1)} %get-tuple-element.98), custom_call_target="InvertDiagBlocksLowerTriangular" | custom-call | tf_op jit(solution)/shard_map/jit(cholesky)/cholesky/custom-call.12 | solution.py:88
  148.7 11.7 %cholesky.394 = f32[128,128]{1,0:T(8,128)S(1)} custom-call(f32[128,128]{1,0:T(8,128)S(1)} %convolution_subtract_fusion.10), custom_call_target="Cholesky" | custom-call | tf_op jit(solution)/shard_map/jit(cholesky)/cholesky | solution.py:88
  166.0 7.0 %while.4 = (s32[]{:T(128)}, f32[256,256]{1,0:T(8,128)}, s32[2,2]{1,0:T(2,128)}, f32[2,128,128]{2,1,0:T(8,128)S(1)}, s32[]{:T(128)}) while((s32[]{:T(128)}, f32[256,256]{1,0:T(8,128)}, s32[2,2]{1,0:T(2,128)}, f32[2,128,128]{2,1,0:T(8,128)S(1)}, s32[]{:T(128)}) %tuple.91), condition=%wide.while_cond.1, body=%wide.while_body.1.sunk | while | flops 2 | bytes 131189 | solution.py:32
  167.3 2.2 bitcast_dynamic-update-slice_fusion.8
  173.7 20.9 %custom-call.51 = f32[2,128,128]{1,2,0:T(8,128)S(1)} custom-call(f32[2,128,128]{2,1,0:T(8,128)} %copy-done.18), custom_call_target="InvertDiagBlocksLowerTriangular" | custom-call | tf_op jit(solution)/shard_map/jit(_solve_triangular)/triangular_solve | solution.py:32
  201.8 2.7 collective-permute-start.4
  206.0 22.0 %collective-permute-done.8 = f32[32,256]{1,0:T(8,128)S(1)} collective-permute-done((f32[32,256]{1,0:T(8,128)S(1)}, f32[32,256]{1,0:T(8,128)S(1)}, u32[]{:S(2)}, u32[]{:S(2)}) %collective-permute-start.8) | collective-permute-done | bytes 32800 | tf_op jit(solution)/shard_map/ppermute | solution.py:15
  230.3 20.5 %collective-permute-done.4 = f32[512,512]{1,0:T(8,128)} collective-permute-done((f32[512,512]{1,0:T(8,128)}, f32[512,512]{1,0:T(8,128)}, u32[]{:S(2)}, u32[]{:S(2)}) %collective-permute-start.4) | collective-permute-done | bytes 1048608 | tf_op jit(solution)/shard_map/ppermute | solution.py:15
  256.7 2.4 collective-permute-start.6
  259.1 15.8 %collective-permute-done.10 = f32[64,512]{0,1:T(8,128)S(1)} collective-permute-done((f32[64,512]{0,1:T(8,128)S(1)}, f32[64,512]{0,1:T(8,128)S(1)}, u32[]{:S(2)}, u32[]{:S(2)}) %collective-permute-start.10) | collective-permute-done | bytes 131104 | tf_op jit(solution)/shard_map/ppermute | solution.py:15
  276.8 3.7 collective-permute-done.6
  282.5 29.8 %collective-permute-done.11 = f32[64,1024]{0,1:T(8,128)} collective-permute-done((f32[64,1024]{0,1:T(8,128)}, f32[64,1024]{0,1:T(8,128)}, u32[]{:S(2)}, u32[]{:S(2)}) %collective-permute-start.11) | collective-permute-done | bytes 262176 | tf_op jit(solution)/shard_map/ppermute | solution.py:15
  314.5 9.0 %collective-permute-done.7 = f32[2,512,128]{2,1,0:T(8,128)} collective-permute-done((f32[2,512,128]{2,1,0:T(8,128)}, f32[2,512,128]{2,1,0:T(8,128)}, u32[]{:S(2)}, u32[]{:S(2)}) %collective-permute-start.7) | collective-permute-done | bytes 524320 | tf_op jit(solution)/shard_map/ppermute | solution.py:15
  329.8 2.4 pad_maximum_fusion
  332.2 5.3 reshape.155
  337.4 18.1 %fusion.7 = f32[4,128,4,128,12]{3,4,2,1,0:T(8,128)} fusion(f32[4,12,4,1,1]{1,2,4,3,0:T(4,128)S(1)} %copy-done.24, f32[4,4,128,4,128]{4,3,2,1,0:T(4,128)} %reshape.155), kind=kOutput, calls=%fused_computation.13 | convolution fusion | flops 150994944 | bytes 16777984 | tf_op jit(solution)/shard_map/cps,c...sltm,cqt->...plqm/dot_general | solution.py:71
  355.5 29.9 %fusion.4 = f32[12,128,12,128]{3,2,0,1:T(8,128)} fusion(f32[4,12,4,1,1]{1,2,0,4,3:T(4,128)S(1)} %copy-done.22, f32[4,128,4,128,12]{3,4,2,1,0:T(8,128)} %fusion.7), kind=kOutput, calls=%fused_computation.11 | convolution fusion | flops 452984832 | bytes 22020864 | tf_op jit(solution)/shard_map/cps,c...sltm,cqt->...plqm/dot_general | solution.py:71
  385.5 10.4 %copy.83 = f32[12,128,12,128]{3,2,1,0:T(8,128)} copy(f32[12,128,12,128]{3,2,0,1:T(8,128)} %fusion.4) | data formatting | bytes 18874368 | tf_op jit(solution)/shard_map/cps,c...sltm,cqt->...plqm/transpose | solution.py:71
  395.9 9.3 %copy.138 = f32[192,8,12,128]{3,1,2,0:T(8,128)S(1)} copy(f32[192,8,12,128]{3,2,1,0:T(8,128)} %bitcast.260) | data formatting | bytes 18874368
  405.2 3.6 copy-done
  411.7 11.7 %cholesky.167 = f32[128,128]{1,0:T(8,128)S(1)} custom-call(f32[128,128]{1,0:T(8,128)S(1)} %cholesky.413), custom_call_target="Cholesky" | custom-call | tf_op jit(solution)/shard_map/jit(cholesky)/cholesky | solution.py:158
  423.5 9.9 %custom-call.52 = f32[1,128,128]{1,2,0:T(8,128)S(1)} custom-call(f32[1,128,128]{2,1,0:T(8,128)S(1)} %get-tuple-element.92), custom_call_target="InvertDiagBlocksLowerTriangular" | custom-call | tf_op jit(solution)/shard_map/jit(cholesky)/cholesky | solution.py:158
  436.7 11.7 %cholesky.190 = f32[128,128]{1,0:T(8,128)S(1)} custom-call(f32[128,128]{1,0:T(8,128)S(1)} %cholesky.417), custom_call_target="Cholesky" | custom-call | tf_op jit(solution)/shard_map/jit(cholesky)/cholesky | solution.py:158
  448.4 9.8 %custom-call.53 = f32[1,128,128]{1,2,0:T(8,128)S(1)} custom-call(f32[1,128,128]{2,1,0:T(8,128)S(1)} %get-tuple-element.89), custom_call_target="InvertDiagBlocksLowerTriangular" | custom-call | tf_op jit(solution)/shard_map/jit(cholesky)/cholesky | solution.py:158
  460.7 11.7 %cholesky.294 = f32[128,128]{1,0:T(8,128)S(1)} custom-call(f32[128,128]{1,0:T(8,128)S(1)} %cholesky.422), custom_call_target="Cholesky" | custom-call | tf_op jit(solution)/shard_map/jit(cholesky)/cholesky | solution.py:158
  472.5 10.0 %custom-call.61 = f32[1,128,128]{1,2,0:T(8,128)S(1)} custom-call(f32[1,128,128]{2,1,0:T(8,128)S(1)} %get-tuple-element.86), custom_call_target="InvertDiagBlocksLowerTriangular" | custom-call | tf_op jit(solution)/shard_map/jit(cholesky)/cholesky/custom-call.12 | solution.py:158
  483.9 11.7 %cholesky.307 = f32[128,128]{1,0:T(8,128)S(1)} custom-call(f32[128,128]{1,0:T(8,128)S(1)} %convolution_subtract_fusion.13), custom_call_target="Cholesky" | custom-call | tf_op jit(solution)/shard_map/jit(cholesky)/cholesky | solution.py:158
  501.9 13.9 %while.5 = (s32[]{:T(128)}, f32[512,512]{1,0:T(8,128)}, s32[4,2]{0,1:T(2,128)S(1)}, f32[4,128,128]{2,1,0:T(8,128)}, s32[]{:T(128)}) while((s32[]{:T(128)}, f32[512,512]{1,0:T(8,128)}, s32[4,2]{0,1:T(2,128)S(1)}, f32[4,128,128]{2,1,0:T(8,128)}, s32[]{:T(128)}) %tuple.88), condition=%wide.while_cond.2, body=%wide.while_body.2.sunk | while | flops 2 | bytes 132205 | solution.py:32
  502.5 2.9 bitcast_dynamic-update-slice_fusion.9
  506.0 2.9 bitcast_dynamic-update-slice_fusion.9
  509.5 2.9 bitcast_dynamic-update-slice_fusion.9
  512.9 2.8 bitcast_dynamic-update-slice_fusion.9
  515.8 41.1 %custom-call.54 = f32[4,128,128]{1,2,0:T(8,128)} custom-call(f32[4,128,128]{2,1,0:T(8,128)} %get-tuple-element.27), custom_call_target="InvertDiagBlocksLowerTriangular" | custom-call | tf_op jit(solution)/shard_map/jit(_solve_triangular)/triangular_solve | solution.py:32
  556.9 3.5 fusion.16
  (223 shorter events, 98.3 us)
Async XLA Ops:
  7.7 64.7 %copy-start.13 = (f32[1,1,256,256]{3,2,1,0:T(8,128)S(1)}, f32[1,1,256,256]{3,2,1,0:T(8,128)}, u32[]{:S(2)}) copy-start(f32[1,1,256,256]{3,2,1,0:T(8,128)} %param.14) | copy-start | bytes 786436
  8.9 64.1 %copy-start.17 = (f32[1,1,512,128]{3,2,1,0:T(8,128)S(1)}, f32[1,1,512,128]{3,2,1,0:T(8,128)}, u32[]{:S(2)}) copy-start(f32[1,1,512,128]{3,2,1,0:T(8,128)} %param.17) | copy-start | bytes 786436
  9.0 66.6 %copy-start.6 = (f32[1,1,256,256]{3,2,1,0:T(8,128)S(1)}, f32[1,1,256,256]{3,2,1,0:T(8,128)}, u32[]{:S(2)}) copy-start(f32[1,1,256,256]{3,2,1,0:T(8,128)} %param.15) | copy-start | bytes 786436
  50.1 0.6 copy-start.25
  72.0 14.1 %copy-start.20 = (f32[4,12,4,1]{1,2,0,3:T(4,128)S(1)}, f32[4,12,4,1]{1,2,0,3:T(4,128)}, u32[]{:S(2)}) copy-start(f32[4,12,4,1]{1,2,0,3:T(4,128)} %constant.417) | copy-start | bytes 2308
  73.1 4.9 collective-permute-start.2
  75.7 7.7 %collective-permute-start = (f32[256,256]{1,0:T(8,128)S(1)}, f32[256,256]{1,0:T(8,128)S(1)}, u32[]{:S(2)}, u32[]{:S(2)}) collective-permute-start(f32[256,256]{1,0:T(8,128)S(1)} %slice_subtract_fusion.2), channel_id=1, source_target_pairs={{0,8},{8,0},{16,24},{24,16},{32,40},{40,32},{48,56},{56,48},{64,72... | collective-permute-start | bytes 786440 | tf_op jit(solution)/shard_map/ppermute | solution.py:15
  78.0 8.1 %collective-permute-start.3 = (f32[2,256,128]{2,1,0:T(8,128)S(1)}, f32[2,256,128]{2,1,0:T(8,128)S(1)}, u32[]{:S(2)}, u32[]{:S(2)}) collective-permute-start(f32[2,256,128]{2,1,0:T(8,128)S(1)} %pad_maximum_fusion.11), channel_id=1, source_target_pairs={{0,1},{1,0},{2,3},{3,2},{4,5},{5,4},{6,7},{7,6},{8,9},{9,8},{10,11... | collective-permute-start | bytes 786440 | tf_op jit(solution)/shard_map/ppermute | solution.py:15
  83.5 4.6 collective-permute-start.1
  87.3 0.8 copy-start.10
  87.3 4.5 copy-start.23
  91.8 8.2 %copy-start.22 = (f32[4,12,4,1,1]{1,2,0,4,3:T(4,128)S(1)}, f32[4,12,4,1,1]{1,2,0,4,3:T(4,128)}, u32[]{:S(2)}) copy-start(f32[4,12,4,1,1]{1,2,0,4,3:T(4,128)} %constant.416) | copy-start | bytes 2308
  122.4 0.7 copy-start.14
  173.0 0.7 copy-start.18
  196.8 7.7 %copy-start.21 = (f32[32,256]{1,0:T(8,128)S(1)}, f32[32,256]{1,0:T(8,128)}, u32[]{:S(2)}) copy-start(f32[32,256]{1,0:T(8,128)} %param.18) | copy-start | bytes 98308
  200.4 1.4 copy-start.1
  201.8 49.0 %collective-permute-start.4 = (f32[512,512]{1,0:T(8,128)}, f32[512,512]{1,0:T(8,128)}, u32[]{:S(2)}, u32[]{:S(2)}) collective-permute-start(f32[512,512]{1,0:T(8,128)} %slice_subtract_fusion), channel_id=1, source_target_pairs={{0,16},{8,24},{16,0},{24,8},{32,48},{40,56},{48,32},{56,40},{64,80... | collective-permute-start | bytes 3145736 | tf_op jit(solution)/shard_map/ppermute | solution.py:15
  204.5 23.4 %collective-permute-start.8 = (f32[32,256]{1,0:T(8,128)S(1)}, f32[32,256]{1,0:T(8,128)S(1)}, u32[]{:S(2)}, u32[]{:S(2)}) collective-permute-start(f32[32,256]{1,0:T(8,128)S(1)} %copy-done.21), channel_id=1, source_target_pairs={{0,8},{8,0},{16,24},{24,16},{32,40},{40,32},{48,56},{56,48},{64,72... | collective-permute-start | bytes 98312 | tf_op jit(solution)/shard_map/ppermute | solution.py:15
  228.1 2.1 collective-permute-start.9
  230.3 25.3 %copy-start.11 = (f32[12,64,128]{2,0,1:T(8,128)S(1)}, f32[12,64,128]{2,0,1:T(8,128)}, u32[]{:S(2)}) copy-start(f32[12,64,128]{2,0,1:T(8,128)} %copy-done.10) | copy-start | bytes 1179652
  254.1 73.5 %collective-permute-start.5 = (f32[2,512,512]{2,1,0:T(8,128)}, f32[2,512,512]{2,1,0:T(8,128)}, u32[]{:S(2)}, u32[]{:S(2)}) collective-permute-start(f32[2,512,512]{2,1,0:T(8,128)} %pad_maximum_fusion.1), channel_id=1, source_target_pairs={{0,2},{1,3},{2,0},{3,1},{4,6},{5,7},{6,4},{7,5},{8,10},{9,11},{10,... | collective-permute-start | bytes 6291464 | tf_op jit(solution)/shard_map/ppermute | solution.py:15
  255.5 19.4 %collective-permute-start.10 = (f32[64,512]{0,1:T(8,128)S(1)}, f32[64,512]{0,1:T(8,128)S(1)}, u32[]{:S(2)}, u32[]{:S(2)}) collective-permute-start(f32[64,512]{0,1:T(8,128)S(1)} %pad_maximum_fusion.12), channel_id=1, source_target_pairs={{0,16},{8,24},{16,0},{24,8},{32,48},{40,56},{48,32},{56,40},{64,80... | collective-permute-start | bytes 393224 | tf_op jit(solution)/shard_map/ppermute | solution.py:15
  256.7 23.8 %collective-permute-start.6 = (f32[512,128]{1,0:T(8,128)S(1)}, f32[512,128]{1,0:T(8,128)S(1)}, u32[]{:S(2)}, u32[]{:S(2)}) collective-permute-start(f32[512,128]{1,0:T(8,128)S(1)} %slice_subtract_fusion.1), channel_id=1, source_target_pairs={{0,16},{8,24},{16,0},{24,8},{32,48},{40,56},{48,32},{56,40},{64,80... | collective-permute-start | bytes 786440 | tf_op jit(solution)/shard_map/ppermute | solution.py:15
  275.0 0.7 copy-start.7
  276.5 35.7 %collective-permute-start.11 = (f32[64,1024]{0,1:T(8,128)}, f32[64,1024]{0,1:T(8,128)}, u32[]{:S(2)}, u32[]{:S(2)}) collective-permute-start(f32[64,1024]{0,1:T(8,128)} %pad_maximum_fusion.7), channel_id=1, source_target_pairs={{0,2},{1,3},{2,0},{3,1},{4,6},{5,7},{6,4},{7,5},{8,10},{9,11},{10,... | collective-permute-start | bytes 786440 | tf_op jit(solution)/shard_map/ppermute | solution.py:15
  280.5 0.7 copy-start.8
  280.5 1.6 copy-start.9
  282.1 41.4 %collective-permute-start.7 = (f32[2,512,128]{2,1,0:T(8,128)}, f32[2,512,128]{2,1,0:T(8,128)}, u32[]{:S(2)}, u32[]{:S(2)}) collective-permute-start(f32[2,512,128]{2,1,0:T(8,128)} %pad_maximum_fusion.6), channel_id=1, source_target_pairs={{0,2},{1,3},{2,0},{3,1},{4,6},{5,7},{6,4},{7,5},{8,10},{9,11},{10,... | collective-permute-start | bytes 1572872 | tf_op jit(solution)/shard_map/ppermute | solution.py:15
  332.2 5.3 copy-start.24
  405.2 3.6 copy-start
  410.7 1.0 copy-start.5
  411.6 145.2 %copy-start.2 = (f32[64,1024]{0,1:T(8,128)S(1)}, f32[64,1024]{0,1:T(8,128)}, u32[]{:S(2)}) copy-start(f32[64,1024]{0,1:T(8,128)} %get-tuple-element.64) | copy-start | bytes 786436
  411.6 145.2 %copy-start.3 = (f32[64,1024]{0,1:T(8,128)S(1)}, f32[64,1024]{0,1:T(8,128)}, u32[]{:S(2)}) copy-start(f32[64,1024]{0,1:T(8,128)} %get-tuple-element.65) | copy-start | bytes 786436
  436.0 0.7 copy-start.15
  515.8 47.9 %copy-start.4 = (f32[512,512]{1,0:T(8,128)S(1)}, f32[512,512]{1,0:T(8,128)}, u32[]{:S(2)}) copy-start(f32[512,512]{1,0:T(8,128)} %get-tuple-element.245) | copy-start | bytes 3145732
  556.9 7.1 %copy-start.12 = (f32[4,128,128]{1,2,0:T(8,128)S(1)}, f32[4,128,128]{1,2,0:T(8,128)}, u32[]{:S(2)}) copy-start(f32[4,128,128]{1,2,0:T(8,128)} %custom-call.54) | copy-start | bytes 786436
  556.9 10.3 %copy-start.19 = (f32[4,12,4,1]{1,2,3,0:T(4,128)S(1)}, f32[4,12,4,1]{1,2,3,0:T(4,128)}, u32[]{:S(2)}) copy-start(f32[4,12,4,1]{1,2,3,0:T(4,128)} %constant.414) | copy-start | bytes 2308
  570.6 1.0 copy-start.16
where the time goes:
time: 582 us; the launch traced here: 572 us
  other arithmetic  260 us (45%)
  waiting for transfers between devices  105 us (18%)
  matrix products  103 us (18%)
  local copies, waits for them, and re-layouts  77.8 us (13%)
  starting transfers between devices  19.7 us (3%)
  between operations  7.21 us (1%)
    ppermute x12, waiting for transfers between devices, swapped(): lax.ppermute(x, axis, [(i, i ^ 1 << apart) for i in range(lax.axis_size(a...  105 us
    another operation x8, other arithmetic, solve_factor(): jax.scipy.linalg.solve_triangular(factor, lower_solved, lower=True, trans=1)  84.4 us
    another operation x15, other arithmetic, local(): factor = jnp.linalg.cholesky(assembled[:inside, :inside])  79.3 us
    dot_general x4, matrix products, assemble(): jnp.einsum('cps,c...sltm,cqt->...plqm', placement, blocks, placement, pre...  67.6 us
    another operation x7, other arithmetic, merge_level(): factor = jnp.linalg.cholesky(assembled[..., :inside, :inside])  36.4 us
    another operation x7, other arithmetic, leaf_reduce(): factor = jnp.linalg.cholesky(inner_matrix)  34.7 us
    another operation x24, local copies, waits for them, and re-layouts  24.8 us
    unnamed x62, local copies, waits for them, and re-layouts  23.1 us
  transfers between devices with their start and end apart: 12, of which 9 were waited for; matrix products, arithmetic and copies ran while one was open for 2% of the time, Pallas kernels for 0%

commit v1 on v0

v1 whole, which is shorter than its diff:
```python
import jax
import jax.numpy as jnp
from jax import lax
from jax.experimental import pallas as pl
from jax.experimental.pallas import tpu as pltpu
from jax.sharding import PartitionSpec as P

F32 = jnp.float32
BF16 = jnp.bfloat16
MESH = pl.DeviceIdType.MESH

LEAF_RHO = (255 * 0.003515625) / (255 * 0.003515625 + 256 * 0.000390625) / 1.05
FACE_RHO = 1.0 / 1.05
LEAF_STEPS = 5
FACE_STEPS = 6


def split(x):
    high = x.astype(BF16)
    low = (x - high.astype(F32)).astype(BF16)
    return high, low


def dot(a, b):
    return jnp.dot(a, b, preferred_element_type=F32)


def mm_split(a, b):
    return dot(a[0], b[0]) + (dot(a[0], b[1]) + dot(a[1], b[0]))


def mm(a, b):
    return mm_split(split(a), split(b))


def eye_mask(n):
    return lax.broadcasted_iota(jnp.int32, (n, n), 0) == lax.broadcasted_iota(jnp.int32, (n, n), 1)


def inverse_of(h, rho, steps):
    n = h.shape[0]
    eye = jnp.where(eye_mask(n), 1.0, 0.0).astype(F32)
    t = 1.0 / rho
    s, r = None, h
    for k in range(steps):
        square = 2.0 * t * t
        alpha = square / (square - 1.0)
        last = k == steps - 1
        rs = split(r)
        if s is None:
            s = alpha * (eye + r)
            r = alpha * mm_split(rs, rs) - (alpha - 1.0) * eye
        elif not last:
            ss = split(s)
            p = mm_split((jnp.concatenate([ss[0], rs[0]], 0), jnp.concatenate([ss[1], rs[1]], 0)), rs)
            s = alpha * (s + p[:n])
            r = alpha * p[n:] - (alpha - 1.0) * eye
        else:
            s = alpha * (s + mm_split(split(s), rs))
        t = square - 1.0
    return s


def face_solve(v, right):
    n = v.shape[0]
    on = eye_mask(n)
    d = jnp.sum(jnp.where(on, v, 0.0), axis=1, keepdims=True)
    di = 1.0 / d
    h = jnp.where(on, 0.0, -v * di)
    return mm(inverse_of(h, FACE_RHO, FACE_STEPS), right * di)


def half_swap(x):
    return pltpu.roll(x, 64, 1)


def kernel(ci, cq, co, mg, src, top, out_in, out_b, mloc, gloc, zq, zf, ut, tv, s1m, s1g, st2, r2, st3, r3, st4, r4, ur, dn2, uyi, dn1, uloc,
           send, recv, tvrecv):
    gx, gy = lax.axis_index("gx"), lax.axis_index("gy")
    lx, ly = gx % 4, gy % 4
    x0, y0 = gx - lx, gy - ly
    bx, by, cx, cy = lx % 2, ly % 2, lx // 2, ly // 2
    px, py = (bx + cx) % 2, (by + cy) % 2

    def at(i, j):
        return (x0 + i, y0 + j)

    barrier = pltpu.get_barrier_semaphore()
    for i in range(4):
        for j in range(4):
            if i or j:
                pl.semaphore_signal(barrier, 1, device_id=at((lx + i) % 4, (ly + j) % 4), device_id_type=MESH)

    def remote(k, source, target, device):
        return pltpu.make_async_remote_copy(src_ref=source, dst_ref=target, send_sem=send.at[k], recv_sem=recv.at[k],
                                            device_id=device, device_id_type=MESH)

    mate = (gx, gy + 1 - 2 * by)
    pair = (gx + 1 - 2 * bx, gy)
    side_y = at(lx, 3 - ly)
    side_x = at(3 - lx, ly)

    on_x = 1 - lx // 2
    pl.semaphore_wait(barrier, 15)
    top_sends = []
    for k in range(4):
        dx = on_x * lx * 3 + (1 - on_x) * k
        dy = on_x * k + (1 - on_x) * (lx - 2) * 3
        away = (dx - lx) * (dx - lx) + (dy - ly) * (dy - ly) > 0
        half = pl.ds((k // 2) * 128, 128)
        slot = tv.at[lx // 2, pl.ds(pl.multiple_of(ly * 32, 32), 32), :]
        copy = pltpu.make_async_remote_copy(src_ref=top.at[:, half], dst_ref=slot, send_sem=send.at[k], recv_sem=tvrecv.at[lx // 2, ly],
                                            device_id=at(dx, dy), device_id_type=MESH)
        top_sends.append((away, copy))

        @pl.when(away)
        def _():
            copy.start()

        @pl.when(jnp.logical_not(away))
        def _():
            tv[lx // 2, pl.ds(pl.multiple_of(ly * 32, 32), 32), :] = top[:, half]

    on = eye_mask(256)
    a = ci[...]
    inner = jnp.where(on, 0.0, 0.5 * (a + a.T))
    o = co[...]
    outer = jnp.where(on, 0.0, 0.5 * (o + o.T))
    q = cq[...]
    qt = q.T
    margin = mg[...]
    m_in = jnp.sum(jnp.where(on, jnp.broadcast_to(margin[:, :256], (256, 256)), 0.0), axis=1, keepdims=True)
    m_out = jnp.sum(jnp.where(on, jnp.broadcast_to(margin[:, 256:], (256, 256)), 0.0), axis=1, keepdims=True)
    d_in = (jnp.sum(inner, 1, keepdims=True) + jnp.sum(q, 1, keepdims=True)) * (1.0 + m_in)
    d_out = (jnp.sum(outer, 1, keepdims=True) + jnp.sum(qt, 1, keepdims=True)) * (1.0 + m_out)
    e_out = jnp.where(on, d_out, -outer)
    di = 1.0 / d_in
    s = inverse_of(inner * di, LEAF_RHO, LEAF_STEPS)

    ut[...] = jnp.zeros_like(ut)
    for side in range(2):
        known = (1 - px) if side == 0 else (1 - py)

        @pl.when(known == 1)
        def _():
            origin = (cx if side == 0 else 2 + cy)
            for j in range(4):
                mine = (lx - origin) * (lx - origin) + (ly - j) * (ly - j) > 0

                @pl.when(mine)
                def _():
                    piece = tv.at[side, pl.ds(j * 32, 32), :]
                    pltpu.make_async_remote_copy(src_ref=piece, dst_ref=piece, send_sem=send.at[0], recv_sem=tvrecv.at[side, j],
                                                 device_id=mate, device_id_type=MESH).wait_recv()

            flipped = tv[side].T
            b = by if side == 0 else bx
            part = jnp.where(b == 0, flipped[:64], flipped[64:])
            start = 64 * bx if side == 0 else 128 + 64 * by
            ut[pl.ds(pl.multiple_of(start, 64), 64), :] = part

    u_known = ut[...]
    moved = mm(jnp.concatenate([q, -e_out], 0), u_known)
    f_in = src[:256, :] + moved[:256]
    f_out = src[256:, :] + moved[256:]

    z = mm(s, jnp.concatenate([q, f_in], 1) * di)
    zq[...] = z[:, :256]
    zf[...] = z[:, 256:]
    reduced = mm(qt, z)
    m = e_out - reduced[:, :256]
    g = f_out + reduced[:, 256:]
    t0, t1 = m[:, :128], m[:, 128:]
    t0 = jnp.where(bx == 0, half_swap(t0), t0)
    t1 = jnp.where(by == 0, half_swap(t1), t1)
    m = jnp.concatenate([t0, t1], 1)
    places = (64 * (1 - bx), 64 * bx, 128 + 64 * (1 - by), 128 + 64 * by)
    for k in range(4):
        rows = pl.ds(pl.multiple_of(places[k], 64), 64)
        mloc[rows, :] = m[64 * k : 64 * k + 64]
        gloc[rows, :] = g[64 * k : 64 * k + 64]

    up1 = [
        remote(4, mloc.at[pl.ds(0, 192), :], s1m, mate),
        remote(5, gloc.at[pl.ds(0, 192), :], s1g, mate),
    ]
    lane = lax.broadcasted_iota(jnp.int32, (64, 128), 1)
    left = lane < 64
    zero = jnp.zeros((64, 128), F32)

    down1 = [
        remote(14, ur.at[pl.ds(64, 64), :], dn1.at[pl.ds(0, 64), :], mate),
        remote(15, ur.at[pl.ds(192, 64), :], dn1.at[pl.ds(64, 64), :], mate),
        remote(16, uyi, dn1.at[pl.ds(128, 64), :], mate),
    ]

    @pl.when(py == 0)
    def _():
        for copy in up1:
            copy.start()
        for copy in down1:
            copy.wait_recv()
        uloc[pl.ds(0, 64), :] = dn1[0:64]
        uloc[pl.ds(64, 64), :] = dn1[64:128]
        uloc[pl.ds(128, 64), :] = dn1[128:192]
        uloc[pl.ds(192, 64), :] = zero
        for copy in up1:
            copy.wait_send()

    @pl.when(py == 1)
    def _():
        up1[0].wait_recv()
        up1[1].wait_recv()
        a0, a1 = mloc[:, :128], mloc[:, 128:]
        n0 = s1m[:, :128]

        def left_of(x):
            return jnp.where(left, x, 0.0)

        def wide_root(x0_, x1_):
            return jnp.concatenate([left_of(x0_), left_of(half_swap(x0_)), left_of(half_swap(x1_))], 1)

        def wide_mate(x0_):
            return jnp.concatenate([jnp.where(left, 0.0, half_swap(x0_)), jnp.where(left, 0.0, x0_), zero], 1)

        v1 = a1[128:192, :64] + s1m[128:192, 128:192]
        gt1 = wide_root(a0[128:192], a1[128:192]) + wide_mate(n0[128:192])
        h1 = gloc[128:192, :] + s1g[128:192, :]
        x1 = face_solve(v1, jnp.concatenate([gt1, h1], 1))
        x1r, b1 = x1[:, :384], x1[:, 384:]
        g1 = jnp.concatenate([mloc[0:64, 128:256], s1m[0:64, 128:256], mloc[64:128, 128:256], s1m[64:128, 128:256], mloc[192:256, 128:256]], 0)[:, :64]
        base1 = jnp.concatenate([
            wide_root(a0[0:64], a1[0:64]), wide_mate(n0[0:64]), wide_root(a0[64:128], a1[64:128]), wide_mate(n0[64:128]),
            wide_root(a0[192:256], a1[192:256])], 0)
        p1 = mm(g1, x1)
        m1 = base1 - p1[:, :384]
        h_r = jnp.concatenate([gloc[0:64, :], s1g[0:64, :], gloc[64:128, :], s1g[64:128, :], gloc[192:256, :]], 0)
        f1 = h_r - p1[:, 384:]

        up2 = [
            remote(6, st2.at[pl.ds(0, 128), :], r2.at[pl.ds(0, 128), :], pair),
            remote(7, st2.at[pl.ds(128, 320), :], r2.at[pl.ds(128, 320), :], pair),
        ]
        down2 = [
            remote(12, ur.at[pl.ds(0, 128), :], dn2.at[pl.ds(0, 128), :], pair),
            remote(13, st2.at[pl.ds(0, 64), :], dn2.at[pl.ds(128, 64), :], pair),
        ]

        @pl.when(px == 0)
        def _():
            st2[0:128, :] = m1[0:128, :128]
            up2[0].start()
            st2[128:256, :] = f1[0:128]
            st2[256:320, :] = m1[256:320, :128]
            st2[320:384, :] = half_swap(m1[256:320, 256:])
            st2[384:448, :] = f1[256:320]
            up2[1].start()
            down2[0].wait_recv()
            down2[1].wait_recv()
            ur[0:128, :] = dn2[0:128, :]
            ur[128:256, :] = jnp.zeros((128, 128), F32)
            ur[256:320, :] = dn2[128:192, :]
            up2[0].wait_send()
            up2[1].wait_send()

        @pl.when(px == 1)
        def _():
            up2[0].wait_recv()
            up2[1].wait_recv()
            v2 = m1[0:128, :128] + r2[0:128, :]
            w0 = r2[256:320, :]
            wt0 = jnp.concatenate([zero, w0], 0).T
            gt2 = jnp.concatenate([m1[0:128, 128:256], m1[0:128, 256:] + wt0], 1)
            x2 = face_solve(v2, jnp.concatenate([gt2, f1[0:128] + r2[128:256, :]], 1))
            x2r, b2 = x2[:, :256], x2[:, 256:]
            g2 = jnp.concatenate([m1[128:320, :128], w0], 0)
            base2 = jnp.concatenate([m1[128:320, 128:], jnp.concatenate([zero, r2[320:384, :]], 1)], 0)
            p2 = mm(g2, x2)
            m2 = base2 - p2[:, :256]
            f2 = jnp.concatenate([f1[128:320], r2[384:448, :]], 0) - p2[:, 256:]

            up3 = [remote(8, st3, r3, side_y)]
            st3[0:128, :] = m2[128:, 128:]
            st3[128:256, :] = m2[128:, :128]
            st3[256:384, :] = f2[128:]
            st3[384:512, :] = m2[:128, 128:]
            st3[512:640, :] = m2[:128, :128]
            st3[640:768, :] = f2[:128]
            up3[0].start()
            up3[0].wait_recv()
            v3 = m2[128:, 128:] + r3[0:128, :]
            x3 = face_solve(v3, jnp.concatenate([m2[128:, :128], r3[128:256, :], f2[128:] + r3[256:384, :]], 1))
            x3r, b3 = x3[:, :256], x3[:, 256:]
            p3 = mm(jnp.concatenate([m2[:128, 128:], r3[384:512, :]], 0), x3)
            f3 = jnp.concatenate([f2[:128], r3[640:768, :]], 0) - p3[:, 256:]
            square = jnp.zeros((128, 128), F32)
            base3 = jnp.concatenate([
                jnp.concatenate([m2[:128, :128], square], 1), jnp.concatenate([square, r3[512:640, :]], 1)], 0)
            m3 = base3 - p3[:, :256]

            up4 = [remote(9, st4, r4, side_x)]
            st4[0:256, :] = m3[:, :128]
            st4[256:512, :] = m3[:, 128:]
            st4[512:768, :] = f3
            up4[0].start()
            up4[0].wait_recv()
            v4 = m3 + jnp.concatenate([r4[0:256, :], r4[256:512, :]], 1)
            u_x = face_solve(v4, f3 + r4[512:768, :])
            u_y = b3 - mm(x3r, u_x)
            u_xi = b2 - mm(x2r, jnp.concatenate([u_x[:128], u_y], 0))
            ur[0:128, :] = u_xi
            down2[0].start()
            st2[0:64, :] = u_y[64:]
            down2[1].start()
            ur[128:256, :] = u_x[:128]
            ur[256:320, :] = u_y[:64]
            up3[0].wait_send()
            up4[0].wait_send()
            down2[0].wait_send()
            down2[1].wait_send()

        ur[320:384, :] = zero
        down1[0].start()
        down1[1].start()
        u_yi = b1 - mm(x1r, ur[...])
        uyi[...] = u_yi
        down1[2].start()
        uloc[0:64, :] = ur[0:64, :]
        uloc[64:128, :] = ur[128:192, :]
        uloc[128:192, :] = u_yi
        uloc[192:256, :] = ur[256:320, :]
        for copy in down1:
            copy.wait_send()

    u_free = jnp.concatenate([uloc[pl.ds(pl.multiple_of(p, 64), 64), :] for p in places], 0)
    out_b[...] = u_free + u_known
    out_in[...] = zf[...] + mm(zq[...], u_free)
    for away, copy in top_sends:

        @pl.when(away)
        def _():
            copy.wait_send()


def solution(mesh):
    def local(couple_inner, couple_cross, couple_outer, margin, sources, top_values):
        vmem = pl.BlockSpec(memory_space=pltpu.VMEM)
        interior, boundary = pl.pallas_call(
            kernel,
            out_shape=(jax.ShapeDtypeStruct((256, 128), F32), jax.ShapeDtypeStruct((256, 128), F32)),
            in_specs=[vmem] * 6,
            out_specs=(vmem, vmem),
            scratch_shapes=[
                pltpu.VMEM((256, 256), F32),
                pltpu.VMEM((256, 128), F32),
                pltpu.VMEM((256, 256), F32),
                pltpu.VMEM((256, 128), F32),
                pltpu.VMEM((256, 128), F32),
                pltpu.VMEM((2, 128, 128), F32),
                pltpu.VMEM((192, 256), F32),
                pltpu.VMEM((192, 128), F32),
                pltpu.VMEM((448, 128), F32),
                pltpu.VMEM((448, 128), F32),
                pltpu.VMEM((768, 128), F32),
                pltpu.VMEM((768, 128), F32),
                pltpu.VMEM((768, 128), F32),
                pltpu.VMEM((768, 128), F32),
                pltpu.VMEM((384, 128), F32),
                pltpu.VMEM((192, 128), F32),
                pltpu.VMEM((64, 128), F32),
                pltpu.VMEM((192, 128), F32),
                pltpu.VMEM((256, 128), F32),
                pltpu.SemaphoreType.DMA((17,)),
                pltpu.SemaphoreType.DMA((17,)),
                pltpu.SemaphoreType.DMA((2, 4)),
            ],
            compiler_params=pltpu.CompilerParams(collective_id=0, has_side_effects=True),
        )(
            couple_inner.reshape(256, 256),
            couple_cross.reshape(256, 256),
            couple_outer.reshape(256, 256),
            margin.reshape(1, 512),
            sources.reshape(512, 128),
            top_values,
        )
        return interior[None, None], boundary[None, None]

    spec = P("gx", "gy", None, None)
    return jax.shard_map(
        local,
        mesh=mesh,
        in_specs=(spec, spec, spec, P("gx", "gy", None), spec, P("gy", "gx")),
        out_specs=(spec, spec),
        check_vma=False,
    )
```

time: 582 us -> 48.8 us (0.08); the launches traced: 572 us -> 48.7 us
  other arithmetic: 260 us -> 0 us
  waiting for transfers between devices: 105 us -> 0 us
  matrix products: 103 us -> 0 us
  local copies, waits for them, and re-layouts: 77.8 us -> 2.26 us
  Pallas kernels: 0 us -> 45.8 us
  starting transfers between devices: 19.7 us -> 0 us
  between operations: 7.21 us -> 0.65 us
    another operation x49 -> x0, other arithmetic: 243 us -> none  [the longest x8 84.4 us: solve_factor(): jax.scipy.linalg.solve_triangular(factor, lower_solved, lower=True, trans=1)]
    ppermute x12 -> x0, waiting for transfers between devices: 105 us -> none  [swapped(): lax.ppermute(x, axis, [(i, i ^ 1 << apart) for i in range(lax.axis_size(a...]
    dot_general x13 -> x0, matrix products: 80.4 us -> none  [the longest x4 67.6 us: assemble(): jnp.einsum('cps,c...sltm,cqt->...plqm', placement, blocks, placement, pre...]
    pallas_call x0 -> x1, Pallas kernels: none -> 45.8 us  [local(): pl.pallas_call(kernel, out_shape=(jax.ShapeDtypeStruct((256, 128), F32),...]
    another operation x36 -> x0, local copies, waits for them, and re-layouts: 26 us -> none
    another operation x36 -> x0, matrix products: 22.5 us -> none  [the longest x13 7.68 us: solve_factor(): jax.scipy.linalg.solve_triangular(factor, right_side, lower=True)]
    unnamed x62 -> x4, local copies, waits for them, and re-layouts: 23.1 us -> 2.26 us
    ppermute x12 -> x0, starting transfers between devices: 19.7 us -> none  [swapped(): lax.ppermute(x, axis, [(i, i ^ 1 << apart) for i in range(lax.axis_size(a...]
  transfers between devices with their start and end apart: 12 -> 0, of which waited for: 9 -> 0; matrix products, arithmetic and copies ran while one was open for 2% -> 0% of each run, Pallas kernels for 0% -> 0%
where the time goes in v1:
time: 48.8 us; the launch traced here: 48.7 us
  Pallas kernels  45.8 us (94%)
  local copies, waits for them, and re-layouts  2.26 us (5%)
  between operations  0.65 us (1%)
    pallas_call x1, Pallas kernels, local(): pl.pallas_call(kernel, out_shape=(jax.ShapeDtypeStruct((256, 128), F32),...  45.8 us
    unnamed x4, local copies, waits for them, and re-layouts  2.26 us

profile of v1, /device:TPU:1, one launch (start us, length us, event | category | flops | bytes accessed | tf_op | source)
XLA Modules:
  0.0 48.7 jit_solution(2787540262307844528)
XLA Ops:
  0.6 45.8 %shard_map.77 = (f32[256,128]{1,0:T(8,128)}, f32[256,128]{1,0:T(8,128)}) custom-call(f32[256,256]{1,0:T(8,128)} %bitcast.7, f32[256,256]{1,0:T(8,128)} %bitcast.8, f32[256,256]{1,0:T(8,128)} %bitcast.9, f32[1,512]{1,0:T(1,128)} %bitcast.13, f32[512,128]{1,0:T(8,128)} %bitcast.10, f32[32,256]{1,0:T(8,128)} %top.1), custom_call_target="tpu_custom_call" | custom-call | tf_op jit(solution)/shard_map/pallas_call | solution.py:348
  46.4 0.0 copy-start
  46.4 1.6 %copy.10 = f32[1,1,256,128]{3,2,1,0:T(8,128)} copy(f32[1,1,256,128]{3,2,1,0:T(8,128)} %bitcast.12) | data formatting | bytes 262144
  48.0 0.0 copy-done
  48.0 0.7 %copy.11 = f32[1,1,256,128]{3,2,1,0:T(8,128)} copy(f32[1,1,256,128]{3,2,1,0:T(8,128)S(1)} %bitcast.11) | data formatting | bytes 262144
Async XLA Ops:
  46.4 1.6 %copy-start = (f32[256,128]{1,0:T(8,128)S(1)}, f32[256,128]{1,0:T(8,128)}, u32[]{:S(2)}) copy-start(f32[256,128]{1,0:T(8,128)} %get-tuple-element.5) | copy-start | bytes 393220

commit v2 on v1

v2 whole, which is shorter than its diff:
```python
import jax
import jax.numpy as jnp
from jax import lax
from jax.experimental import pallas as pl
from jax.experimental.pallas import tpu as pltpu
from jax.sharding import PartitionSpec as P

F32 = jnp.float32
BF16 = jnp.bfloat16
MESH = pl.DeviceIdType.MESH

LEAF_RHO = (255 * 0.003515625) / (255 * 0.003515625 + 256 * 0.000390625) / 1.05
FACE_RHO = 1.0 / 1.05
LEAF_STEPS = 5
FACE_STEPS = 6


def split(x):
    high = x.astype(BF16)
    low = (x - high.astype(F32)).astype(BF16)
    return high, low


def dot(a, b):
    return jnp.dot(a, b, preferred_element_type=F32)


def mm_split(a, b):
    return dot(a[0], b[0]) + (dot(a[0], b[1]) + dot(a[1], b[0]))


def mm(a, b):
    return mm_split(split(a), split(b))


def eye_mask(n):
    return lax.broadcasted_iota(jnp.int32, (n, n), 0) == lax.broadcasted_iota(jnp.int32, (n, n), 1)


def inverse_of(h, rho, steps):
    n = h.shape[0]
    eye = jnp.where(eye_mask(n), 1.0, 0.0).astype(F32)
    t = 1.0 / rho
    s, r = None, h
    for k in range(steps):
        square = 2.0 * t * t
        alpha = square / (square - 1.0)
        last = k == steps - 1
        rs = split(r)
        if s is None:
            s = alpha * (eye + r)
            r = alpha * mm_split(rs, rs) - (alpha - 1.0) * eye
        elif not last:
            ss = split(s)
            p = mm_split((jnp.concatenate([ss[0], rs[0]], 0), jnp.concatenate([ss[1], rs[1]], 0)), rs)
            s = alpha * (s + p[:n])
            r = alpha * p[n:] - (alpha - 1.0) * eye
        else:
            s = alpha * (s + mm_split(split(s), rs))
        t = square - 1.0
    return s


def face_inverse(v):
    n = v.shape[0]
    on = eye_mask(n)
    di = 1.0 / jnp.sum(jnp.where(on, v, 0.0), axis=1, keepdims=True)
    h = jnp.where(on, 0.0, -v * di)
    return inverse_of(h, FACE_RHO, FACE_STEPS), di


def half_swap(x):
    return pltpu.roll(x, 64, 1)


def cat(*parts, axis=0):
    return jnp.concatenate(parts, axis)


def kernel(ci_h, cq_h, co_h, mg_h, src_h, top, out_in, out_b, ci, cq, co, mg, src, mloc, gloc, ut, tv, s1m, s1g, st2, r2, st3, r3, st4, r4, ur,
           dnst, dn2, uyi, dn1, uloc, load, send, recv, tvrecv):
    gx, gy = lax.axis_index("gx"), lax.axis_index("gy")
    lx, ly = gx % 4, gy % 4
    x0, y0 = gx - lx, gy - ly
    bx, by, cx, cy = lx % 2, ly % 2, lx // 2, ly // 2
    px, py = (bx + cx) % 2, (by + cy) % 2

    def at(i, j):
        return (x0 + i, y0 + j)

    barrier = pltpu.get_barrier_semaphore()
    for i in range(4):
        for j in range(4):
            if i or j:
                pl.semaphore_signal(barrier, 1, device_id=at((lx + i) % 4, (ly + j) % 4), device_id_type=MESH)

    loads = [pltpu.make_async_copy(h, v, load.at[k]) for k, (h, v) in enumerate(((ci_h, ci), (cq_h, cq), (mg_h, mg), (co_h, co), (src_h, src)))]
    for copy in loads:
        copy.start()

    def remote(k, source, target, device):
        return pltpu.make_async_remote_copy(src_ref=source, dst_ref=target, send_sem=send.at[k], recv_sem=recv.at[k],
                                            device_id=device, device_id_type=MESH)

    def rows(ref, start, count):
        return ref.at[pl.ds(start, count), :]

    mate = (gx, gy + 1 - 2 * by)
    pair = (gx + 1 - 2 * bx, gy)
    side_y = at(lx, 3 - ly)
    side_x = at(3 - lx, ly)

    on = eye_mask(256)
    loads[0].wait()
    a = ci[...]
    inner = jnp.where(on, 0.0, 0.5 * (a + a.T))
    loads[1].wait()
    loads[2].wait()
    q = cq[...]
    margin = mg[...]
    m_in = jnp.sum(jnp.where(on, jnp.broadcast_to(margin[:, :256], (256, 256)), 0.0), axis=1, keepdims=True)
    m_out = jnp.sum(jnp.where(on, jnp.broadcast_to(margin[:, 256:], (256, 256)), 0.0), axis=1, keepdims=True)
    d_in = (jnp.sum(inner, 1, keepdims=True) + jnp.sum(q, 1, keepdims=True)) * (1.0 + m_in)
    di = 1.0 / d_in

    pl.semaphore_wait(barrier, 15)
    on_x = 1 - lx // 2
    top_sends = []
    for k in range(4):
        dx = on_x * lx * 3 + (1 - on_x) * k
        dy = on_x * k + (1 - on_x) * (lx - 2) * 3
        away = (dx - lx) * (dx - lx) + (dy - ly) * (dy - ly) > 0
        piece = top.at[:, pl.ds((k // 2) * 128, 128)]
        slot = tv.at[lx // 2, pl.ds(pl.multiple_of(ly * 32, 32), 32), :]
        copy = pltpu.make_async_remote_copy(src_ref=piece, dst_ref=slot, send_sem=send.at[k], recv_sem=tvrecv.at[lx // 2, ly],
                                            device_id=at(dx, dy), device_id_type=MESH)
        here = pltpu.make_async_copy(piece, slot, load.at[5])
        top_sends.append((away, copy, here))

        @pl.when(away)
        def _():
            copy.start()

        @pl.when(jnp.logical_not(away))
        def _():
            here.start()

    s = inverse_of(inner * di, LEAF_RHO, LEAF_STEPS)
    qt = q.T
    loads[3].wait()
    o = co[...]
    outer = jnp.where(on, 0.0, 0.5 * (o + o.T))
    d_out = (jnp.sum(outer, 1, keepdims=True) + jnp.sum(qt, 1, keepdims=True)) * (1.0 + m_out)
    e_out = jnp.where(on, d_out, -outer)
    zq = mm(s, q * di)
    m = e_out - mm(qt, zq)
    t0, t1 = m[:, :128], m[:, 128:]
    t0 = jnp.where(bx == 0, half_swap(t0), t0)
    t1 = jnp.where(by == 0, half_swap(t1), t1)
    places = [pl.multiple_of(p, 64) for p in (64 * (1 - bx), 64 * bx, 128 + 64 * (1 - by), 128 + 64 * by)]
    for k in range(4):
        mloc[pl.ds(places[k], 64), :] = cat(t0[64 * k : 64 * k + 64], t1[64 * k : 64 * k + 64], axis=1)

    def leaf_flux():
        ut[...] = jnp.zeros_like(ut)
        for away, _, here in top_sends:

            @pl.when(jnp.logical_not(away))
            def _():
                here.wait()

        for side in range(2):
            known = (1 - px) if side == 0 else (1 - py)

            @pl.when(known == 1)
            def _():
                origin = cx if side == 0 else 2 + cy
                for j in range(4):
                    mine = (lx - origin) * (lx - origin) + (ly - j) * (ly - j) > 0

                    @pl.when(mine)
                    def _():
                        piece = tv.at[side, pl.ds(j * 32, 32), :]
                        pltpu.make_async_remote_copy(src_ref=piece, dst_ref=piece, send_sem=send.at[0], recv_sem=tvrecv.at[side, j],
                                                     device_id=mate, device_id_type=MESH).wait_recv()

                flipped = tv[side].T
                b = by if side == 0 else bx
                part = jnp.where(b == 0, flipped[:64], flipped[64:])
                start = 64 * bx if side == 0 else 128 + 64 * by
                ut[pl.ds(pl.multiple_of(start, 64), 64), :] = part

        loads[4].wait()
        moved = mm(cat(q, -e_out), ut[...])
        z = mm(s, (src[:256, :] + moved[:256]) * di)
        g = src[256:, :] + moved[256:] + mm(qt, z)
        for k in range(4):
            gloc[pl.ds(places[k], 64), :] = g[64 * k : 64 * k + 64]
        src[:256, :] = z

    up1 = [
        remote(4, rows(mloc, 128, 64), rows(s1m, 128, 64), mate),
        remote(5, rows(mloc, 0, 128), rows(s1m, 0, 128), mate),
        remote(6, rows(gloc, 0, 192), s1g, mate),
    ]
    down1 = [
        remote(7, rows(ur, 64, 64), rows(dn1, 0, 64), mate),
        remote(8, rows(ur, 192, 64), rows(dn1, 64, 64), mate),
        remote(9, uyi, rows(dn1, 128, 64), mate),
    ]
    left = lax.broadcasted_iota(jnp.int32, (64, 128), 1) < 64
    zero = jnp.zeros((64, 128), F32)

    @pl.when(py == 0)
    def _():
        up1[0].start()
        up1[1].start()
        leaf_flux()
        up1[2].start()
        for copy in down1:
            copy.wait_recv()
        uloc[0:192, :] = dn1[...]
        uloc[192:256, :] = zero
        for copy in up1:
            copy.wait_send()

    @pl.when(py == 1)
    def _():
        up1[0].wait_recv()
        v1 = mloc[128:192, 128:256] + s1m[128:192, 128:256]
        k1, d1 = face_inverse(v1[:, :64])
        leaf_flux()
        up1[1].wait_recv()

        def left_of(x):
            return jnp.where(left, x, 0.0)

        def wide_root(k):
            x, y = mloc[k : k + 64, :128], mloc[k : k + 64, 128:]
            return cat(left_of(x), left_of(half_swap(x)), left_of(half_swap(y)), axis=1)

        def wide_mate(k):
            x = s1m[k : k + 64, :128]
            return cat(jnp.where(left, 0.0, half_swap(x)), jnp.where(left, 0.0, x), zero, axis=1)

        gt1 = wide_root(128) + wide_mate(128)
        g1 = cat(mloc[0:64, 128:256], s1m[0:64, 128:256], mloc[64:128, 128:256], s1m[64:128, 128:256], mloc[192:256, 128:256])[:, :64]
        base1 = cat(wide_root(0), wide_mate(0), wide_root(64), wide_mate(64), wide_root(192))
        up1[2].wait_recv()
        x1 = mm(k1, cat(gt1, gloc[128:192, :] + s1g[128:192, :], axis=1) * d1)
        x1r, b1 = x1[:, :384], x1[:, 384:]
        p1 = mm(g1, x1)
        m1 = base1 - p1[:, :384]
        f1 = cat(gloc[0:64, :], s1g[0:64, :], gloc[64:128, :], s1g[64:128, :], gloc[192:256, :]) - p1[:, 384:]

        up2 = [
            remote(10, rows(st2, 0, 128), rows(r2, 0, 128), pair),
            remote(11, rows(st2, 128, 128), rows(r2, 128, 128), pair),
            remote(12, rows(st2, 256, 192), rows(r2, 256, 192), pair),
        ]
        down2 = [remote(13, dnst, dn2, pair)]

        @pl.when(px == 0)
        def _():
            st2[0:128, :] = m1[0:128, :128]
            up2[0].start()
            st2[128:192, :] = m1[256:320, :128]
            st2[192:256, :] = half_swap(m1[256:320, 256:])
            up2[1].start()
            st2[256:384, :] = f1[0:128]
            st2[384:448, :] = f1[256:320]
            up2[2].start()
            down2[0].wait_recv()
            ur[0:128, :] = dn2[0:128, :]
            ur[128:256, :] = jnp.zeros((128, 128), F32)
            ur[256:320, :] = dn2[128:192, :]
            for copy in up2:
                copy.wait_send()

        @pl.when(px == 1)
        def _():
            up2[0].wait_recv()
            k2, d2 = face_inverse(m1[0:128, :128] + r2[0:128, :])
            up2[1].wait_recv()
            w0 = r2[128:192, :]
            gt2 = cat(m1[0:128, 128:256], m1[0:128, 256:] + cat(zero, w0).T, axis=1)
            base2 = cat(m1[128:320, 128:], cat(zero, r2[192:256, :], axis=1))
            up2[2].wait_recv()
            x2 = mm(k2, cat(gt2, f1[0:128] + r2[256:384, :], axis=1) * d2)
            x2r, b2 = x2[:, :256], x2[:, 256:]

            up3 = [
                remote(14, rows(st3, 0, 128), rows(r3, 0, 128), side_y),
                remote(15, rows(st3, 128, 256), rows(r3, 128, 256), side_y),
                remote(16, rows(st3, 384, 128), rows(r3, 384, 128), side_y),
                remote(17, rows(st3, 512, 128), rows(r3, 512, 128), side_y),
            ]
            p2y = mm(cat(m1[256:320, :128], w0), x2)
            m2y = base2[128:] - p2y[:, :256]
            f2y = cat(f1[256:320], r2[384:448, :]) - p2y[:, 256:]
            st3[0:128, :] = m2y[:, 128:]
            up3[0].start()
            st3[128:256, :] = m2y[:, :128]
            st3[256:384, :] = f2y
            up3[1].start()
            p2x = mm(m1[128:256, :128], x2)
            m2x = base2[:128] - p2x[:, :256]
            f2x = f1[128:256] - p2x[:, 256:]
            st3[384:512, :] = m2x[:, :128]
            up3[2].start()
            st3[512:640, :] = f2x
            up3[3].start()
            up3[0].wait_recv()
            k3, d3 = face_inverse(m2y[:, 128:] + r3[0:128, :])
            up3[1].wait_recv()
            yx = r3[128:256, :]
            x3 = mm(k3, cat(m2y[:, :128], yx, f2y + r3[256:384, :], axis=1) * d3)
            x3r, b3 = x3[:, :256], x3[:, 256:]
            p3 = mm(cat(m2x[:, 128:], yx.T), x3)
            up3[2].wait_recv()

            up4 = [
                remote(18, rows(st4, 0, 384), rows(r4, 0, 384), side_x),
                remote(19, rows(st4, 384, 256), rows(r4, 384, 256), side_x),
            ]
            m00, m01, m11 = m2x[:, :128] - p3[:128, :128], -p3[:128, 128:256], r3[384:512, :] - p3[128:, 128:256]
            st4[0:128, :] = m00
            st4[128:256, :] = m01
            st4[256:384, :] = m11
            up4[0].start()
            up3[3].wait_recv()
            f3 = cat(f2x, r3[512:640, :]) - p3[:, 256:]
            st4[384:640, :] = f3
            up4[1].start()
            back = mm(x2r[:, 128:], x3)
            down_map = cat(x3r, cat(x2r[:, :128], jnp.zeros((128, 128), F32), axis=1) - back[:, :256])
            down_free = cat(b3, b2 - back[:, 256:])
            up4[0].wait_recv()
            v01 = m01 + r4[128:256, :]
            k4, d4 = face_inverse(cat(cat(m00 + r4[0:128, :], v01, axis=1), cat(v01.T, m11 + r4[256:384, :], axis=1)))
            up4[1].wait_recv()
            u_x = mm(k4, (f3 + r4[384:640, :]) * d4)
            u_low = down_free - mm(down_map, u_x)
            dnst[0:128, :] = u_low[128:]
            dnst[128:192, :] = u_low[64:128]
            down2[0].start()
            ur[0:128, :] = u_low[128:]
            ur[128:256, :] = u_x[:128]
            ur[256:320, :] = u_low[:64]
            for copy in up3 + up4 + down2:
                copy.wait_send()

        ur[320:384, :] = zero
        down1[0].start()
        down1[1].start()
        u_yi = b1 - mm(x1r, ur[...])
        uyi[...] = u_yi
        down1[2].start()
        uloc[0:64, :] = ur[0:64, :]
        uloc[64:128, :] = ur[128:192, :]
        uloc[128:192, :] = u_yi
        uloc[192:256, :] = ur[256:320, :]
        for copy in down1:
            copy.wait_send()

    u_free = cat(*[uloc[pl.ds(p, 64), :] for p in places])
    out_b[...] = u_free + ut[...]
    out_in[...] = src[:256, :] + mm(zq, u_free)
    for away, copy, _ in top_sends:

        @pl.when(away)
        def _():
            copy.wait_send()


def solution(mesh):
    def local(couple_inner, couple_cross, couple_outer, margin, sources, top_values):
        vmem = pl.BlockSpec(memory_space=pltpu.VMEM)
        anywhere = pl.BlockSpec(memory_space=pl.ANY)
        shapes = [(256, 256)] * 3 + [(1, 512), (512, 128), (256, 256), (256, 128), (256, 128), (2, 128, 128), (192, 256), (192, 128),
                  (448, 128), (448, 128), (640, 128), (640, 128), (640, 128), (640, 128), (384, 128), (192, 128), (192, 128), (64, 128),
                  (192, 128), (256, 128)]
        dma = pltpu.SemaphoreType.DMA
        interior, boundary = pl.pallas_call(
            kernel,
            out_shape=(pltpu.VMEM((256, 128), F32), pltpu.VMEM((256, 128), F32)),
            in_specs=[anywhere] * 6,
            out_specs=(vmem, vmem),
            scratch_shapes=[pltpu.VMEM(shape, F32) for shape in shapes] + [dma((6,)), dma((20,)), dma((20,)), dma((2, 4))],
            compiler_params=pltpu.CompilerParams(collective_id=0, has_side_effects=True),
        )(
            couple_inner.reshape(256, 256),
            couple_cross.reshape(256, 256),
            couple_outer.reshape(256, 256),
            margin.reshape(1, 512),
            sources.reshape(512, 128),
            top_values,
        )
        return interior[None, None], boundary[None, None]

    spec = P("gx", "gy", None, None)
    return jax.shard_map(
        local,
        mesh=mesh,
        in_specs=(spec, spec, spec, P("gx", "gy", None), spec, P("gy", "gx")),
        out_specs=(spec, spec),
        check_vma=False,
    )
```

time: 48.8 us -> 37.9 us (0.78)
  Pallas kernels: 45.8 us -> 35.9 us
  local copies, waits for them, and re-layouts: 2.26 us -> 1.31 us
    pallas_call x1, Pallas kernels: 45.8 us -> 35.9 us  [local(): pl.pallas_call(kernel, out_shape=(pltpu.VMEM((256, 128), F32), pltpu.VMEM...]
    unnamed x4 -> x2, local copies, waits for them, and re-layouts: 2.26 us -> 1.31 us
where the time goes in v2:
time: 37.9 us; the launch traced here: 37.8 us
  Pallas kernels  35.9 us (95%)
  local copies, waits for them, and re-layouts  1.31 us (3%)
  between operations  0.64 us (2%)
    pallas_call x1, Pallas kernels, local(): pl.pallas_call(kernel, out_shape=(pltpu.VMEM((256, 128), F32), pltpu.VMEM...  35.9 us
    unnamed x2, local copies, waits for them, and re-layouts  1.31 us

profile of v2, /device:TPU:1, one launch (start us, length us, event | category | flops | bytes accessed | tf_op | source)
XLA Modules:
  0.0 37.8 jit_solution(8151460839692255335)
XLA Ops:
  0.6 35.9 %shard_map.77 = (f32[256,128]{1,0:T(8,128)S(1)}, f32[256,128]{1,0:T(8,128)S(1)}) custom-call(f32[256,256]{1,0:T(8,128)} %bitcast.9, f32[256,256]{1,0:T(8,128)} %bitcast.10, f32[256,256]{1,0:T(8,128)} %bitcast.11, f32[1,512]{1,0:T(1,128)} %bitcast.13, f32[512,128]{1,0:T(8,128)} %bitcast.12, f32[32,256]{1,0:T(8,128)} %top.1), custom_call_target="tpu_custom_call" | custom-call | tf_op jit(solution)/shard_map/pallas_call | solution.py:384
  36.5 0.7 %copy.10 = f32[1,1,256,128]{3,2,1,0:T(8,128)} copy(f32[1,1,256,128]{3,2,1,0:T(8,128)S(1)} %bitcast.8) | data formatting | bytes 262144
  37.2 0.7 %copy.11 = f32[1,1,256,128]{3,2,1,0:T(8,128)} copy(f32[1,1,256,128]{3,2,1,0:T(8,128)S(1)} %bitcast.7) | data formatting | bytes 262144

commit v3 on v2

--- a/solution.py
+++ b/solution.py
@@ -26,7 +26,9 @@
 
 
 def mm_split(a, b):
-    return dot(a[0], b[0]) + (dot(a[0], b[1]) + dot(a[1], b[0]))
+    if a[0].shape[1] % 128:
+        return dot(a[0], b[0]) + (dot(a[0], b[1]) + dot(a[1], b[0]))
+    return dot(jnp.concatenate([a[0], a[0], a[1]], 1), jnp.concatenate([b[0], b[1], b[0]], 0))
 
 
 def mm(a, b):
@@ -45,18 +47,22 @@
     for k in range(steps):
         square = 2.0 * t * t
         alpha = square / (square - 1.0)
-        last = k == steps - 1
-        rs = split(r)
-        if s is None:
+        if k == steps - 1:
+            s = alpha * (s + dot(s.astype(BF16), r.astype(BF16)))
+        elif k == steps - 2:
+            rs = split(r)
+            p = mm_split(split(s), rs)
+            r = alpha * dot(rs[0], rs[0]) - (alpha - 1.0) * eye
+            s = alpha * (s + p)
+        elif s is None:
+            rs = split(r)
             s = alpha * (eye + r)
             r = alpha * mm_split(rs, rs) - (alpha - 1.0) * eye
-        elif not last:
-            ss = split(s)
+        else:
+            ss, rs = split(s), split(r)
             p = mm_split((jnp.concatenate([ss[0], rs[0]], 0), jnp.concatenate([ss[1], rs[1]], 0)), rs)
             s = alpha * (s + p[:n])
             r = alpha * p[n:] - (alpha - 1.0) * eye
-        else:
-            s = alpha * (s + mm_split(split(s), rs))
         t = square - 1.0
     return s
 
@@ -78,7 +84,7 @@
 
 
 def kernel(ci_h, cq_h, co_h, mg_h, src_h, top, out_in, out_b, ci, cq, co, mg, src, mloc, gloc, ut, tv, s1m, s1g, st2, r2, st3, r3, st4, r4, ur,
-           dnst, dn2, uyi, dn1, uloc, load, send, recv, tvrecv):
+           dnst, dn2, uyi, dn1, uloc, x1b, load, send, recv, tvrecv):
     gx, gy = lax.axis_index("gx"), lax.axis_index("gy")
     lx, ly = gx % 4, gy % 4
     x0, y0 = gx - lx, gy - ly
@@ -122,6 +128,8 @@
     m_out = jnp.sum(jnp.where(on, jnp.broadcast_to(margin[:, 256:], (256, 256)), 0.0), axis=1, keepdims=True)
     d_in = (jnp.sum(inner, 1, keepdims=True) + jnp.sum(q, 1, keepdims=True)) * (1.0 + m_in)
     di = 1.0 / d_in
+
+    s = inverse_of(inner * di, LEAF_RHO, LEAF_STEPS)
 
     pl.semaphore_wait(barrier, 15)
     on_x = 1 - lx // 2
@@ -145,7 +153,6 @@
         def _():
             here.start()
 
-    s = inverse_of(inner * di, LEAF_RHO, LEAF_STEPS)
     qt = q.T
     loads[3].wait()
     o = co[...]
@@ -229,7 +236,6 @@
         up1[0].wait_recv()
         v1 = mloc[128:192, 128:256] + s1m[128:192, 128:256]
         k1, d1 = face_inverse(v1[:, :64])
-        leaf_flux()
         up1[1].wait_recv()
 
         def left_of(x):
@@ -246,12 +252,15 @@
         gt1 = wide_root(128) + wide_mate(128)
         g1 = cat(mloc[0:64, 128:256], s1m[0:64, 128:256], mloc[64:128, 128:256], s1m[64:128, 128:256], mloc[192:256, 128:256])[:, :64]
         base1 = cat(wide_root(0), wide_mate(0), wide_root(64), wide_mate(64), wide_root(192))
-        up1[2].wait_recv()
-        x1 = mm(k1, cat(gt1, gloc[128:192, :] + s1g[128:192, :], axis=1) * d1)
-        x1r, b1 = x1[:, :384], x1[:, 384:]
-        p1 = mm(g1, x1)
-        m1 = base1 - p1[:, :384]
-        f1 = cat(gloc[0:64, :], s1g[0:64, :], gloc[64:128, :], s1g[64:128, :], gloc[192:256, :]) - p1[:, 384:]
+        x1r = mm(k1, gt1 * d1)
+        m1 = base1 - mm(g1, x1r)
+
+        def flux1():
+            leaf_flux()
+            up1[2].wait_recv()
+            b1 = mm(k1, (gloc[128:192, :] + s1g[128:192, :]) * d1)
+            x1b[...] = b1
+            return cat(gloc[0:64, :], s1g[0:64, :], gloc[64:128, :], s1g[64:128, :], gloc[192:256, :]) - mm(g1, b1)
 
         up2 = [
             remote(10, rows(st2, 0, 128), rows(r2, 0, 128), pair),
@@ -267,6 +276,7 @@
             st2[128:192, :] = m1[256:320, :128]
             st2[192:256, :] = half_swap(m1[256:320, 256:])
             up2[1].start()
+            f1 = flux1()
             st2[256:384, :] = f1[0:128]
             st2[384:448, :] = f1[256:320]
             up2[2].start()
@@ -279,60 +289,61 @@
 
         @pl.when(px == 1)
         def _():
+            f1 = flux1()
             up2[0].wait_recv()
             k2, d2 = face_inverse(m1[0:128, :128] + r2[0:128, :])
             up2[1].wait_recv()
             w0 = r2[128:192, :]
             gt2 = cat(m1[0:128, 128:256], m1[0:128, 256:] + cat(zero, w0).T, axis=1)
-            base2 = cat(m1[128:320, 128:], cat(zero, r2[192:256, :], axis=1))
-            up2[2].wait_recv()
-            x2 = mm(k2, cat(gt2, f1[0:128] + r2[256:384, :], axis=1) * d2)
-            x2r, b2 = x2[:, :256], x2[:, 256:]
+            x2r = mm(k2, gt2 * d2)
 
             up3 = [
                 remote(14, rows(st3, 0, 128), rows(r3, 0, 128), side_y),
-                remote(15, rows(st3, 128, 256), rows(r3, 128, 256), side_y),
-                remote(16, rows(st3, 384, 128), rows(r3, 384, 128), side_y),
-                remote(17, rows(st3, 512, 128), rows(r3, 512, 128), side_y),
+                remote(15, rows(st3, 128, 128), rows(r3, 128, 128), side_y),
+                remote(16, rows(st3, 256, 128), rows(r3, 256, 128), side_y),
+                remote(17, rows(st3, 384, 256), rows(r3, 384, 256), side_y),
             ]
-            p2y = mm(cat(m1[256:320, :128], w0), x2)
-            m2y = base2[128:] - p2y[:, :256]
-            f2y = cat(f1[256:320], r2[384:448, :]) - p2y[:, 256:]
+            g2y = cat(m1[256:320, :128], w0)
+            m2y = cat(m1[256:320, 128:], cat(zero, r2[192:256, :], axis=1)) - mm(g2y, x2r)
             st3[0:128, :] = m2y[:, 128:]
             up3[0].start()
             st3[128:256, :] = m2y[:, :128]
-            st3[256:384, :] = f2y
             up3[1].start()
-            p2x = mm(m1[128:256, :128], x2)
-            m2x = base2[:128] - p2x[:, :256]
-            f2x = f1[128:256] - p2x[:, 256:]
-            st3[384:512, :] = m2x[:, :128]
+            g2x = m1[128:256, :128]
+            m2x = m1[128:256, 128:] - mm(g2x, x2r)
+            st3[256:384, :] = m2x[:, :128]
             up3[2].start()
+            up2[2].wait_recv()
+            b2 = mm(k2, (f1[0:128] + r2[256:384, :]) * d2)
+            f2y = cat(f1[256:320], r2[384:448, :]) - mm(g2y, b2)
+            f2x = f1[128:256] - mm(g2x, b2)
+            st3[384:512, :] = f2y
             st3[512:640, :] = f2x
             up3[3].start()
             up3[0].wait_recv()
             k3, d3 = face_inverse(m2y[:, 128:] + r3[0:128, :])
             up3[1].wait_recv()
             yx = r3[128:256, :]
-            x3 = mm(k3, cat(m2y[:, :128], yx, f2y + r3[256:384, :], axis=1) * d3)
-            x3r, b3 = x3[:, :256], x3[:, 256:]
-            p3 = mm(cat(m2x[:, 128:], yx.T), x3)
+            x3r = mm(k3, cat(m2y[:, :128], yx, axis=1) * d3)
+            g3 = cat(m2x[:, 128:], yx.T)
+            p3 = mm(g3, x3r)
             up3[2].wait_recv()
 
             up4 = [
                 remote(18, rows(st4, 0, 384), rows(r4, 0, 384), side_x),
                 remote(19, rows(st4, 384, 256), rows(r4, 384, 256), side_x),
             ]
-            m00, m01, m11 = m2x[:, :128] - p3[:128, :128], -p3[:128, 128:256], r3[384:512, :] - p3[128:, 128:256]
+            m00, m01, m11 = m2x[:, :128] - p3[:128, :128], -p3[:128, 128:], r3[256:384, :] - p3[128:, 128:]
             st4[0:128, :] = m00
             st4[128:256, :] = m01
             st4[256:384, :] = m11
             up4[0].start()
             up3[3].wait_recv()
-            f3 = cat(f2x, r3[512:640, :]) - p3[:, 256:]
+            b3 = mm(k3, (f2y + r3[384:512, :]) * d3)
+            f3 = cat(f2x, r3[512:640, :]) - mm(g3, b3)
             st4[384:640, :] = f3
             up4[1].start()
-            back = mm(x2r[:, 128:], x3)
+            back = mm(x2r[:, 128:], cat(x3r, b3, axis=1))
             down_map = cat(x3r, cat(x2r[:, :128], jnp.zeros((128, 128), F32), axis=1) - back[:, :256])
             down_free = cat(b3, b2 - back[:, 256:])
             up4[0].wait_recv()
@@ -353,7 +364,7 @@
         ur[320:384, :] = zero
         down1[0].start()
         down1[1].start()
-        u_yi = b1 - mm(x1r, ur[...])
+        u_yi = x1b[...] - mm(x1r, ur[...])
         uyi[...] = u_yi
         down1[2].start()
         uloc[0:64, :] = ur[0:64, :]
@@ -379,7 +390,7 @@
         anywhere = pl.BlockSpec(memory_space=pl.ANY)
         shapes = [(256, 256)] * 3 + [(1, 512), (512, 128), (256, 256), (256, 128), (256, 128), (2, 128, 128), (192, 256), (192, 128),
                   (448, 128), (448, 128), (640, 128), (640, 128), (640, 128), (640, 128), (384, 128), (192, 128), (192, 128), (64, 128),
-                  (192, 128), (256, 128)]
+                  (192, 128), (256, 128), (64, 128)]
         dma = pltpu.SemaphoreType.DMA
         interior, boundary = pl.pallas_call(
             kernel,

time: 37.9 us -> 34 us (0.90)
  Pallas kernels: 35.9 us -> 32 us
    pallas_call x1, Pallas kernels: 35.9 us -> 32 us  [local(): pl.pallas_call(kernel, out_shape=(pltpu.VMEM((256, 128), F32), pltpu.VMEM...]
where the time goes in v3:
time: 34 us; the launch traced here: 33.9 us
  Pallas kernels  32 us (94%)
  local copies, waits for them, and re-layouts  1.31 us (4%)
  between operations  0.64 us (2%)
    pallas_call x1, Pallas kernels, local(): pl.pallas_call(kernel, out_shape=(pltpu.VMEM((256, 128), F32), pltpu.VMEM...  32 us
    unnamed x2, local copies, waits for them, and re-layouts  1.31 us

profile of v3, /device:TPU:1, one launch (start us, length us, event | category | flops | bytes accessed | tf_op | source)
XLA Modules:
  0.0 33.9 jit_solution(15661110747187601210)
XLA Ops:
  0.6 32.0 %shard_map.77 = (f32[256,128]{1,0:T(8,128)S(1)}, f32[256,128]{1,0:T(8,128)S(1)}) custom-call(f32[256,256]{1,0:T(8,128)} %bitcast.9, f32[256,256]{1,0:T(8,128)} %bitcast.10, f32[256,256]{1,0:T(8,128)} %bitcast.11, f32[1,512]{1,0:T(1,128)} %bitcast.13, f32[512,128]{1,0:T(8,128)} %bitcast.12, f32[32,256]{1,0:T(8,128)} %top.1), custom_call_target="tpu_custom_call" | custom-call | tf_op jit(solution)/shard_map/pallas_call | solution.py:395
  32.6 0.7 %copy.10 = f32[1,1,256,128]{3,2,1,0:T(8,128)} copy(f32[1,1,256,128]{3,2,1,0:T(8,128)S(1)} %bitcast.8) | data formatting | bytes 262144
  33.3 0.7 %copy.11 = f32[1,1,256,128]{3,2,1,0:T(8,128)} copy(f32[1,1,256,128]{3,2,1,0:T(8,128)S(1)} %bitcast.7) | data formatting | bytes 262144

commit v4 on v3

--- a/solution.py
+++ b/solution.py
@@ -26,8 +26,16 @@
 
 
 def mm_split(a, b):
-    if a[0].shape[1] % 128:
+    depth, width = b[0].shape
+    if depth % 128:
         return dot(a[0], b[0]) + (dot(a[0], b[1]) + dot(a[1], b[0]))
+    if width == 128 and depth == 128:
+        wide = jnp.concatenate([b[0], b[1]], 1)
+        out = dot(jnp.concatenate([a[0], a[1]], 1), jnp.concatenate([wide, wide], 0))
+        return out[:, :128] + out[:, 128:]
+    if width == 128:
+        out = dot(a[0], jnp.concatenate([b[0], b[1]], 1))
+        return out[:, :128] + (out[:, 128:] + dot(a[1], b[0]))
     return dot(jnp.concatenate([a[0], a[0], a[1]], 1), jnp.concatenate([b[0], b[1], b[0]], 0))
 
 
@@ -67,12 +75,12 @@
     return s
 
 
-def face_inverse(v):
+def face_inverse(v, rho=FACE_RHO, steps=FACE_STEPS):
     n = v.shape[0]
     on = eye_mask(n)
     di = 1.0 / jnp.sum(jnp.where(on, v, 0.0), axis=1, keepdims=True)
     h = jnp.where(on, 0.0, -v * di)
-    return inverse_of(h, FACE_RHO, FACE_STEPS), di
+    return inverse_of(h, rho, steps), di
 
 
 def half_swap(x):
@@ -85,6 +93,10 @@
 
 def kernel(ci_h, cq_h, co_h, mg_h, src_h, top, out_in, out_b, ci, cq, co, mg, src, mloc, gloc, ut, tv, s1m, s1g, st2, r2, st3, r3, st4, r4, ur,
            dnst, dn2, uyi, dn1, uloc, x1b, load, send, recv, tvrecv):
+    loads = [pltpu.make_async_copy(h, v, load.at[k]) for k, (h, v) in enumerate(((ci_h, ci), (cq_h, cq), (mg_h, mg), (co_h, co), (src_h, src)))]
+    for copy in loads:
+        copy.start()
+
     gx, gy = lax.axis_index("gx"), lax.axis_index("gy")
     lx, ly = gx % 4, gy % 4
     x0, y0 = gx - lx, gy - ly
@@ -99,10 +111,6 @@
         for j in range(4):
             if i or j:
                 pl.semaphore_signal(barrier, 1, device_id=at((lx + i) % 4, (ly + j) % 4), device_id_type=MESH)
-
-    loads = [pltpu.make_async_copy(h, v, load.at[k]) for k, (h, v) in enumerate(((ci_h, ci), (cq_h, cq), (mg_h, mg), (co_h, co), (src_h, src)))]
-    for copy in loads:
-        copy.start()
 
     def remote(k, source, target, device):
         return pltpu.make_async_remote_copy(src_ref=source, dst_ref=target, send_sem=send.at[k], recv_sem=recv.at[k],
@@ -129,7 +137,18 @@
     d_in = (jnp.sum(inner, 1, keepdims=True) + jnp.sum(q, 1, keepdims=True)) * (1.0 + m_in)
     di = 1.0 / d_in
 
-    s = inverse_of(inner * di, LEAF_RHO, LEAF_STEPS)
+    qt = q.T
+    loads[3].wait()
+    o = co[...]
+    outer = jnp.where(on, 0.0, 0.5 * (o + o.T))
+    d_out = (jnp.sum(outer, 1, keepdims=True) + jnp.sum(qt, 1, keepdims=True)) * (1.0 + m_out)
+    e_out = jnp.where(on, d_out, -outer)
+
+    di0 = di[:128]
+    s0 = inverse_of(inner[:128, :128] * di0, LEAF_RHO, LEAF_STEPS)
+    first = mm(s0, cat(inner[:128, 128:], q[:128], axis=1) * di0)
+    across, across_t = first[:, :128], inner[128:, :128]
+    second = mm(across_t, first)
 
     pl.semaphore_wait(barrier, 15)
     on_x = 1 - lx // 2
@@ -153,13 +172,13 @@
         def _():
             here.start()
 
-    qt = q.T
-    loads[3].wait()
-    o = co[...]
-    outer = jnp.where(on, 0.0, 0.5 * (o + o.T))
-    d_out = (jnp.sum(outer, 1, keepdims=True) + jnp.sum(qt, 1, keepdims=True)) * (1.0 + m_out)
-    e_out = jnp.where(on, d_out, -outer)
-    zq = mm(s, q * di)
+    s1, di1 = face_inverse(jnp.where(on[:128, :128], d_in[128:], 0.0) - inner[128:, 128:] - second[:, :128], LEAF_RHO, LEAF_STEPS)
+
+    def leaf_solve(y0, rest):
+        z1 = mm(s1, rest * di1)
+        return cat(y0 + mm(across, z1), z1)
+
+    zq = leaf_solve(first[:, 128:], q[128:] + second[:, 128:])
     m = e_out - mm(qt, zq)
     t0, t1 = m[:, :128], m[:, 128:]
     t0 = jnp.where(bx == 0, half_swap(t0), t0)
@@ -167,43 +186,6 @@
     places = [pl.multiple_of(p, 64) for p in (64 * (1 - bx), 64 * bx, 128 + 64 * (1 - by), 128 + 64 * by)]
     for k in range(4):
         mloc[pl.ds(places[k], 64), :] = cat(t0[64 * k : 64 * k + 64], t1[64 * k : 64 * k + 64], axis=1)
-
-    def leaf_flux():
-        ut[...] = jnp.zeros_like(ut)
-        for away, _, here in top_sends:
-
-            @pl.when(jnp.logical_not(away))
-            def _():
-                here.wait()
-
-        for side in range(2):
-            known = (1 - px) if side == 0 else (1 - py)
-
-            @pl.when(known == 1)
-            def _():
-                origin = cx if side == 0 else 2 + cy
-                for j in range(4):
-                    mine = (lx - origin) * (lx - origin) + (ly - j) * (ly - j) > 0
-
-                    @pl.when(mine)
-                    def _():
-                        piece = tv.at[side, pl.ds(j * 32, 32), :]
-                        pltpu.make_async_remote_copy(src_ref=piece, dst_ref=piece, send_sem=send.at[0], recv_sem=tvrecv.at[side, j],
-                                                     device_id=mate, device_id_type=MESH).wait_recv()
-
-                flipped = tv[side].T
-                b = by if side == 0 else bx
-                part = jnp.where(b == 0, flipped[:64], flipped[64:])
-                start = 64 * bx if side == 0 else 128 + 64 * by
-                ut[pl.ds(pl.multiple_of(start, 64), 64), :] = part
-
-        loads[4].wait()
-        moved = mm(cat(q, -e_out), ut[...])
-        z = mm(s, (src[:256, :] + moved[:256]) * di)
-        g = src[256:, :] + moved[256:] + mm(qt, z)
-        for k in range(4):
-            gloc[pl.ds(places[k], 64), :] = g[64 * k : 64 * k + 64]
-        src[:256, :] = z
 
     up1 = [
         remote(4, rows(mloc, 128, 64), rows(s1m, 128, 64), mate),
@@ -222,6 +204,45 @@
     def _():
         up1[0].start()
         up1[1].start()
+
+    def leaf_flux():
+        loads[4].wait()
+        y0 = mm(s0, src[:128, :] * di0)
+        z = leaf_solve(y0, src[128:256, :] + mm(across_t, y0))
+        g = src[256:, :] + mm(qt, z)
+        for k in range(4):
+            gloc[pl.ds(places[k], 64), :] = g[64 * k : 64 * k + 64]
+        src[:256, :] = z
+        ut[...] = jnp.zeros_like(ut)
+        for away, _, here in top_sends:
+
+            @pl.when(jnp.logical_not(away))
+            def _():
+                here.wait()
+
+        for side in range(2):
+            known = (1 - px) if side == 0 else (1 - py)
+
+            @pl.when(known == 1)
+            def _():
+                origin = cx if side == 0 else 2 + cy
+                for j in range(4):
+                    mine = (lx - origin) * (lx - origin) + (ly - j) * (ly - j) > 0
+
+                    @pl.when(mine)
+                    def _():
+                        piece = tv.at[side, pl.ds(j * 32, 32), :]
+                        pltpu.make_async_remote_copy(src_ref=piece, dst_ref=piece, send_sem=send.at[0], recv_sem=tvrecv.at[side, j],
+                                                     device_id=mate, device_id_type=MESH).wait_recv()
+
+                flipped = tv[side].T
+                b = by if side == 0 else bx
+                ut[64 + 128 * side : 128 + 128 * side, :] = jnp.where(b == 0, flipped[:64], flipped[64:])
+
+        gloc[...] = gloc[...] - mm(mloc[...], ut[...])
+
+    @pl.when(py == 0)
+    def _():
         leaf_flux()
         up1[2].start()
         for copy in down1:
@@ -327,36 +348,54 @@
             x3r = mm(k3, cat(m2y[:, :128], yx, axis=1) * d3)
             g3 = cat(m2x[:, 128:], yx.T)
             p3 = mm(g3, x3r)
+
+            up4 = [
+                remote(18, rows(st4, 0, 136), rows(r4, 0, 136), side_x),
+                remote(19, rows(st4, 136, 128), rows(r4, 136, 128), side_x),
+                remote(20, rows(st4, 264, 256), rows(r4, 264, 256), side_x),
+            ]
+            m00, m01 = m2x[:, :128] - p3[:128, :128], -p3[:128, 128:]
+            st4[136:264, :] = m01
             up3[2].wait_recv()
-
-            up4 = [
-                remote(18, rows(st4, 0, 384), rows(r4, 0, 384), side_x),
-                remote(19, rows(st4, 384, 256), rows(r4, 384, 256), side_x),
-            ]
-            m00, m01, m11 = m2x[:, :128] - p3[:128, :128], -p3[:128, 128:], r3[256:384, :] - p3[128:, 128:]
-            st4[0:128, :] = m00
-            st4[128:256, :] = m01
-            st4[256:384, :] = m11
+            m11 = r3[256:384, :] - p3[128:, 128:]
+            on128 = eye_mask(128)
+            lower = lax.broadcasted_iota(jnp.int32, (128, 128), 0) >= lax.broadcasted_iota(jnp.int32, (128, 128), 1)
+            st4[0:128, :] = jnp.where(lower, m00, m11)
+            st4[128:136, :] = jnp.broadcast_to(jnp.sum(jnp.where(on128, m11, 0.0), axis=0, keepdims=True), (8, 128))
             up4[0].start()
+            up4[1].start()
             up3[3].wait_recv()
             b3 = mm(k3, (f2y + r3[384:512, :]) * d3)
             f3 = cat(f2x, r3[512:640, :]) - mm(g3, b3)
-            st4[384:640, :] = f3
-            up4[1].start()
+            st4[264:520, :] = f3
+            up4[2].start()
             back = mm(x2r[:, 128:], cat(x3r, b3, axis=1))
-            down_map = cat(x3r, cat(x2r[:, :128], jnp.zeros((128, 128), F32), axis=1) - back[:, :256])
+            near_map = cat(x3r[:, :128], x2r[:, :128] - back[:, :128])
+            far_map = cat(x3r[:, 128:], -back[:, 128:256])
             down_free = cat(b3, b2 - back[:, 256:])
             up4[0].wait_recv()
-            v01 = m01 + r4[128:256, :]
-            k4, d4 = face_inverse(cat(cat(m00 + r4[0:128, :], v01, axis=1), cat(v01.T, m11 + r4[256:384, :], axis=1)))
+            mix = r4[0:128, :]
+            mix_t = mix.T
+            k4, d4 = face_inverse(m00 + jnp.where(lower, mix, mix_t))
             up4[1].wait_recv()
-            u_x = mm(k4, (f3 + r4[384:640, :]) * d4)
-            u_low = down_free - mm(down_map, u_x)
+            v01 = m01 + r4[136:264, :]
+            v10 = v01.T
+            x4 = mm(k4, v01 * d4)
+            far_block = m11 + jnp.where(on128, jnp.broadcast_to(r4[128:129, :], (128, 128)), jnp.where(lower, mix_t, mix))
+            k5, d5 = face_inverse(far_block - mm(v10, x4))
+            x4t = x4.T
+            far_map = far_map - mm(near_map, x4)
+            up4[2].wait_recv()
+            h4 = f3[:128] + r4[264:392, :]
+            y4 = mm(k4, h4 * d4)
+            u_far = mm(k5, (f3[128:] + r4[392:520, :] - mm(x4t, h4)) * d5)
+            u_near = y4 - mm(x4, u_far)
+            u_low = down_free - mm(near_map, y4) - mm(far_map, u_far)
             dnst[0:128, :] = u_low[128:]
             dnst[128:192, :] = u_low[64:128]
             down2[0].start()
             ur[0:128, :] = u_low[128:]
-            ur[128:256, :] = u_x[:128]
+            ur[128:256, :] = u_near
             ur[256:320, :] = u_low[:64]
             for copy in up3 + up4 + down2:
                 copy.wait_send()
@@ -374,14 +413,23 @@
         for copy in down1:
             copy.wait_send()
 
-    u_free = cat(*[uloc[pl.ds(p, 64), :] for p in places])
-    out_b[...] = u_free + ut[...]
-    out_in[...] = src[:256, :] + mm(zq, u_free)
+    uloc[...] = uloc[...] + ut[...]
+    u_b = cat(*[uloc[pl.ds(p, 64), :] for p in places])
+    out_b[...] = u_b
+    out_in[...] = src[:256, :] + mm(zq, u_b)
     for away, copy, _ in top_sends:
 
         @pl.when(away)
         def _():
             copy.wait_send()
+
+
+def store(a, b, out_a, out_b, sem):
+    copies = [pltpu.make_async_copy(x, y, sem.at[k]) for k, (x, y) in enumerate(((a, out_a), (b, out_b)))]
+    for copy in copies:
+        copy.start()
+    for copy in copies:
+        copy.wait()
 
 
 def solution(mesh):
@@ -397,7 +445,7 @@
             out_shape=(pltpu.VMEM((256, 128), F32), pltpu.VMEM((256, 128), F32)),
             in_specs=[anywhere] * 6,
             out_specs=(vmem, vmem),
-            scratch_shapes=[pltpu.VMEM(shape, F32) for shape in shapes] + [dma((6,)), dma((20,)), dma((20,)), dma((2, 4))],
+            scratch_shapes=[pltpu.VMEM(shape, F32) for shape in shapes] + [dma((6,)), dma((22,)), dma((22,)), dma((2, 4))],
             compiler_params=pltpu.CompilerParams(collective_id=0, has_side_effects=True),
         )(
             couple_inner.reshape(256, 256),
@@ -407,6 +455,13 @@
             sources.reshape(512, 128),
             top_values,
         )
+        interior, boundary = pl.pallas_call(
+            store,
+            out_shape=(jax.ShapeDtypeStruct((256, 128), F32),) * 2,
+            in_specs=[vmem, vmem],
+            out_specs=(anywhere, anywhere),
+            scratch_shapes=[dma((2,))],
+        )(pltpu.with_memory_space_constraint(interior, pltpu.VMEM), pltpu.with_memory_space_constraint(boundary, pltpu.VMEM))
         return interior[None, None], boundary[None, None]
 
     spec = P("gx", "gy", None, None)

time: 34 us -> 32.7 us (0.962)
  local copies, waits for them, and re-layouts: 1.31 us -> 0 us
    unnamed x2 -> x0, local copies, waits for them, and re-layouts: 1.31 us -> none
    pallas_call x0 -> x1, Pallas kernels: none -> 0.72 us  [local(): pl.pallas_call(store, out_shape=(jax.ShapeDtypeStruct((256, 128), F32),)...]
    pallas_call x1, Pallas kernels: 32 us -> 31.3 us  [local(): pl.pallas_call(kernel, out_shape=(pltpu.VMEM((256, 128), F32), pltpu.VMEM...]
where the time goes in v4:
time: 32.7 us; the launch traced here: 32.6 us
  Pallas kernels  32 us (98%)
  between operations  0.64 us (2%)
    pallas_call x1, Pallas kernels, local(): pl.pallas_call(kernel, out_shape=(pltpu.VMEM((256, 128), F32), pltpu.VMEM...  31.3 us
    pallas_call x1, Pallas kernels, local(): pl.pallas_call(store, out_shape=(jax.ShapeDtypeStruct((256, 128), F32),)...  0.72 us

profile of v4, /device:TPU:1, one launch (start us, length us, event | category | flops | bytes accessed | tf_op | source)
XLA Modules:
  0.0 32.6 jit_solution(812433046743726973)
XLA Ops:
  0.6 31.3 %shard_map.77 = (f32[256,128]{1,0:T(8,128)S(1)}, f32[256,128]{1,0:T(8,128)S(1)}) custom-call(f32[256,256]{1,0:T(8,128)} %bitcast.7, f32[256,256]{1,0:T(8,128)} %bitcast.8, f32[256,256]{1,0:T(8,128)} %bitcast.9, f32[1,512]{1,0:T(1,128)} %bitcast.11, f32[512,128]{1,0:T(8,128)} %bitcast.10, f32[32,256]{1,0:T(8,128)} %top.1), custom_call_target="tpu_custom_call" | custom-call | tf_op jit(solution)/shard_map/pallas_call | solution.py:443
  31.9 0.7 %shard_map.78 = (f32[256,128]{1,0:T(8,128)}, f32[256,128]{1,0:T(8,128)}) custom-call(f32[256,128]{1,0:T(8,128)S(1)} %get-tuple-element.6.a, f32[256,128]{1,0:T(8,128)S(1)} %get-tuple-element.7.b), custom_call_target="tpu_custom_call" | custom-call | tf_op jit(solution)/shard_map/pallas_call | solution.py:458

commit v5 on v4

--- a/solution.py
+++ b/solution.py
@@ -68,9 +68,9 @@
             r = alpha * mm_split(rs, rs) - (alpha - 1.0) * eye
         else:
             ss, rs = split(s), split(r)
-            p = mm_split((jnp.concatenate([ss[0], rs[0]], 0), jnp.concatenate([ss[1], rs[1]], 0)), rs)
-            s = alpha * (s + p[:n])
-            r = alpha * p[n:] - (alpha - 1.0) * eye
+            p = mm_split((jnp.concatenate([rs[0], ss[0]], 0), jnp.concatenate([rs[1], ss[1]], 0)), rs)
+            r = alpha * p[:n] - (alpha - 1.0) * eye
+            s = alpha * (s + p[n:])
         t = square - 1.0
     return s
 
@@ -136,13 +136,6 @@
     m_out = jnp.sum(jnp.where(on, jnp.broadcast_to(margin[:, 256:], (256, 256)), 0.0), axis=1, keepdims=True)
     d_in = (jnp.sum(inner, 1, keepdims=True) + jnp.sum(q, 1, keepdims=True)) * (1.0 + m_in)
     di = 1.0 / d_in
-
-    qt = q.T
-    loads[3].wait()
-    o = co[...]
-    outer = jnp.where(on, 0.0, 0.5 * (o + o.T))
-    d_out = (jnp.sum(outer, 1, keepdims=True) + jnp.sum(qt, 1, keepdims=True)) * (1.0 + m_out)
-    e_out = jnp.where(on, d_out, -outer)
 
     di0 = di[:128]
     s0 = inverse_of(inner[:128, :128] * di0, LEAF_RHO, LEAF_STEPS)
@@ -172,6 +165,12 @@
         def _():
             here.start()
 
+    qt = q.T
+    loads[3].wait()
+    o = co[...]
+    outer = jnp.where(on, 0.0, 0.5 * (o + o.T))
+    d_out = (jnp.sum(outer, 1, keepdims=True) + jnp.sum(qt, 1, keepdims=True)) * (1.0 + m_out)
+    e_out = jnp.where(on, d_out, -outer)
     s1, di1 = face_inverse(jnp.where(on[:128, :128], d_in[128:], 0.0) - inner[128:, 128:] - second[:, :128], LEAF_RHO, LEAF_STEPS)
 
     def leaf_solve(y0, rest):
@@ -270,11 +269,28 @@
             x = s1m[k : k + 64, :128]
             return cat(jnp.where(left, 0.0, half_swap(x)), jnp.where(left, 0.0, x), zero, axis=1)
 
-        gt1 = wide_root(128) + wide_mate(128)
+        gt1 = (wide_root(128) + wide_mate(128)) * d1
         g1 = cat(mloc[0:64, 128:256], s1m[0:64, 128:256], mloc[64:128, 128:256], s1m[64:128, 128:256], mloc[192:256, 128:256])[:, :64]
-        base1 = cat(wide_root(0), wide_mate(0), wide_root(64), wide_mate(64), wide_root(192))
-        x1r = mm(k1, gt1 * d1)
-        m1 = base1 - mm(g1, x1r)
+        x1a = mm(k1, gt1[:, :128])
+        shared1 = cat(wide_root(0)[:, :128], wide_mate(0)[:, :128]) - mm(g1[:128], x1a)
+        up2 = [
+            remote(10, rows(st2, 0, 128), rows(r2, 0, 128), pair),
+            remote(11, rows(st2, 128, 128), rows(r2, 128, 128), pair),
+            remote(12, rows(st2, 256, 192), rows(r2, 256, 192), pair),
+        ]
+
+        @pl.when(px == 0)
+        def _():
+            st2[0:128, :] = shared1
+            up2[0].start()
+
+        x1b_ = mm(k1, gt1[:, 128:])
+        x1r = cat(x1a, x1b_, axis=1)
+        p1l, p1r = mm(g1[128:], x1a), mm(g1, x1b_)
+        m1 = cat(
+            cat(shared1, cat(wide_root(64)[:, :128], wide_mate(64)[:, :128], wide_root(192)[:, :128]) - p1l),
+            cat(*[w[:, 128:] for w in (wide_root(0), wide_mate(0), wide_root(64), wide_mate(64), wide_root(192))]) - p1r,
+            axis=1)
 
         def flux1():
             leaf_flux()
@@ -283,17 +299,10 @@
             x1b[...] = b1
             return cat(gloc[0:64, :], s1g[0:64, :], gloc[64:128, :], s1g[64:128, :], gloc[192:256, :]) - mm(g1, b1)
 
-        up2 = [
-            remote(10, rows(st2, 0, 128), rows(r2, 0, 128), pair),
-            remote(11, rows(st2, 128, 128), rows(r2, 128, 128), pair),
-            remote(12, rows(st2, 256, 192), rows(r2, 256, 192), pair),
-        ]
         down2 = [remote(13, dnst, dn2, pair)]
 
         @pl.when(px == 0)
         def _():
-            st2[0:128, :] = m1[0:128, :128]
-            up2[0].start()
             st2[128:192, :] = m1[256:320, :128]
             st2[192:256, :] = half_swap(m1[256:320, 256:])
             up2[1].start()
@@ -316,7 +325,7 @@
             up2[1].wait_recv()
             w0 = r2[128:192, :]
             gt2 = cat(m1[0:128, 128:256], m1[0:128, 256:] + cat(zero, w0).T, axis=1)
-            x2r = mm(k2, gt2 * d2)
+            x2y = mm(k2, gt2[:, 128:] * d2)
 
             up3 = [
                 remote(14, rows(st3, 0, 128), rows(r3, 0, 128), side_y),
@@ -325,10 +334,14 @@
                 remote(17, rows(st3, 384, 256), rows(r3, 384, 256), side_y),
             ]
             g2y = cat(m1[256:320, :128], w0)
-            m2y = cat(m1[256:320, 128:], cat(zero, r2[192:256, :], axis=1)) - mm(g2y, x2r)
-            st3[0:128, :] = m2y[:, 128:]
+            base2y = cat(m1[256:320, 128:], cat(zero, r2[192:256, :], axis=1))
+            m2yy = base2y[:, 128:] - mm(g2y, x2y)
+            st3[0:128, :] = m2yy
             up3[0].start()
-            st3[128:256, :] = m2y[:, :128]
+            x2x = mm(k2, gt2[:, :128] * d2)
+            x2r = cat(x2x, x2y, axis=1)
+            m2yx = base2y[:, :128] - mm(g2y, x2x)
+            st3[128:256, :] = m2yx
             up3[1].start()
             g2x = m1[128:256, :128]
             m2x = m1[128:256, 128:] - mm(g2x, x2r)
@@ -342,10 +355,10 @@
             st3[512:640, :] = f2x
             up3[3].start()
             up3[0].wait_recv()
-            k3, d3 = face_inverse(m2y[:, 128:] + r3[0:128, :])
+            k3, d3 = face_inverse(m2yy + r3[0:128, :])
             up3[1].wait_recv()
             yx = r3[128:256, :]
-            x3r = mm(k3, cat(m2y[:, :128], yx, axis=1) * d3)
+            x3r = mm(k3, cat(m2yx, yx, axis=1) * d3)
             g3 = cat(m2x[:, 128:], yx.T)
             p3 = mm(g3, x3r)
 

time: 32.7 us -> 31.8 us (0.972)
  Pallas kernels: 32 us -> 31.1 us
    pallas_call x1, Pallas kernels: 31.3 us -> 30.4 us  [local(): pl.pallas_call(kernel, out_shape=(pltpu.VMEM((256, 128), F32), pltpu.VMEM...]
where the time goes in v5:
time: 31.8 us; the launch traced here: 31.7 us
  Pallas kernels  31.1 us (98%)
  between operations  0.64 us (2%)
    pallas_call x1, Pallas kernels, local(): pl.pallas_call(kernel, out_shape=(pltpu.VMEM((256, 128), F32), pltpu.VMEM...  30.4 us
    pallas_call x1, Pallas kernels, local(): pl.pallas_call(store, out_shape=(jax.ShapeDtypeStruct((256, 128), F32),)...  0.72 us

profile of v5, /device:TPU:1, one launch (start us, length us, event | category | flops | bytes accessed | tf_op | source)
XLA Modules:
  0.0 31.7 jit_solution(9158026145233593560)
XLA Ops:
  0.6 30.4 %shard_map.77 = (f32[256,128]{1,0:T(8,128)S(1)}, f32[256,128]{1,0:T(8,128)S(1)}) custom-call(f32[256,256]{1,0:T(8,128)} %bitcast.7, f32[256,256]{1,0:T(8,128)} %bitcast.8, f32[256,256]{1,0:T(8,128)} %bitcast.9, f32[1,512]{1,0:T(1,128)} %bitcast.11, f32[512,128]{1,0:T(8,128)} %bitcast.10, f32[32,256]{1,0:T(8,128)} %top.1), custom_call_target="tpu_custom_call" | custom-call | tf_op jit(solution)/shard_map/pallas_call | solution.py:456
  31.0 0.7 %shard_map.78 = (f32[256,128]{1,0:T(8,128)}, f32[256,128]{1,0:T(8,128)}) custom-call(f32[256,128]{1,0:T(8,128)S(1)} %get-tuple-element.6.a, f32[256,128]{1,0:T(8,128)S(1)} %get-tuple-element.7.b), custom_call_target="tpu_custom_call" | custom-call | tf_op jit(solution)/shard_map/pallas_call | solution.py:471

commit v6 on v5

--- a/solution.py
+++ b/solution.py
@@ -11,6 +11,10 @@
 
 LEAF_RHO = (255 * 0.003515625) / (255 * 0.003515625 + 256 * 0.000390625) / 1.05
 FACE_RHO = 1.0 / 1.05
+FIRST_RHO = (64 * 9) / (64 * 9 + 192) / 1.05
+SECOND_RHO = (64 * 9) / (64 * 9 + 128) / 1.05
+THIRD_RHO = (64 * 9) / (64 * 9 + 64) / 1.05
+NEAR_STEPS = 5
 LEAF_STEPS = 5
 FACE_STEPS = 6
 
@@ -121,6 +125,7 @@
 
     mate = (gx, gy + 1 - 2 * by)
     pair = (gx + 1 - 2 * bx, gy)
+    cross = (gx + 1 - 2 * bx, gy + 1 - 2 * by)
     side_y = at(lx, 3 - ly)
     side_x = at(3 - lx, ly)
 
@@ -196,6 +201,11 @@
         remote(8, rows(ur, 192, 64), rows(dn1, 64, 64), mate),
         remote(9, uyi, rows(dn1, 128, 64), mate),
     ]
+    down2 = [
+        remote(13, rows(dnst, 0, 64), uyi, pair),
+        remote(22, rows(dnst, 64, 64), rows(dn1, 0, 64), cross),
+        remote(23, rows(dnst, 128, 128), dn2, pair),
+    ]
     left = lax.broadcasted_iota(jnp.int32, (64, 128), 1) < 64
     zero = jnp.zeros((64, 128), F32)
 
@@ -244,9 +254,21 @@
     def _():
         leaf_flux()
         up1[2].start()
-        for copy in down1:
-            copy.wait_recv()
-        uloc[0:192, :] = dn1[...]
+
+        @pl.when(px == 1)
+        def _():
+            down1[0].wait_recv()
+            down1[1].wait_recv()
+            uloc[64:128, :] = dn1[64:128, :]
+
+        @pl.when(px == 0)
+        def _():
+            down2[1].wait_recv()
+            uloc[64:128, :] = zero
+
+        down1[2].wait_recv()
+        uloc[0:64, :] = dn1[0:64, :]
+        uloc[128:192, :] = dn1[128:192, :]
         uloc[192:256, :] = zero
         for copy in up1:
             copy.wait_send()
@@ -255,7 +277,7 @@
     def _():
         up1[0].wait_recv()
         v1 = mloc[128:192, 128:256] + s1m[128:192, 128:256]
-        k1, d1 = face_inverse(v1[:, :64])
+        k1, d1 = face_inverse(v1[:, :64], FIRST_RHO, NEAR_STEPS)
         up1[1].wait_recv()
 
         def left_of(x):
@@ -277,6 +299,7 @@
             remote(10, rows(st2, 0, 128), rows(r2, 0, 128), pair),
             remote(11, rows(st2, 128, 128), rows(r2, 128, 128), pair),
             remote(12, rows(st2, 256, 192), rows(r2, 256, 192), pair),
+            remote(21, rows(st2, 448, 192), rows(r2, 448, 192), pair),
         ]
 
         @pl.when(px == 0)
@@ -299,8 +322,6 @@
             x1b[...] = b1
             return cat(gloc[0:64, :], s1g[0:64, :], gloc[64:128, :], s1g[64:128, :], gloc[192:256, :]) - mm(g1, b1)
 
-        down2 = [remote(13, dnst, dn2, pair)]
-
         @pl.when(px == 0)
         def _():
             st2[128:192, :] = m1[256:320, :128]
@@ -310,10 +331,18 @@
             st2[256:384, :] = f1[0:128]
             st2[384:448, :] = f1[256:320]
             up2[2].start()
+            st2[448:512, :] = x1a
+            st2[512:576, :] = half_swap(x1r[:, 256:])
+            st2[576:640, :] = x1b[...]
+            up2[3].start()
             down2[0].wait_recv()
-            ur[0:128, :] = dn2[0:128, :]
-            ur[128:256, :] = jnp.zeros((128, 128), F32)
-            ur[256:320, :] = dn2[128:192, :]
+            down1[2].start()
+            down2[2].wait_recv()
+            uloc[0:64, :] = dn2[0:64, :]
+            uloc[64:128, :] = zero
+            uloc[128:192, :] = uyi[...]
+            uloc[192:256, :] = dn2[64:128, :]
+            down1[2].wait_send()
             for copy in up2:
                 copy.wait_send()
 
@@ -321,7 +350,7 @@
         def _():
             f1 = flux1()
             up2[0].wait_recv()
-            k2, d2 = face_inverse(m1[0:128, :128] + r2[0:128, :])
+            k2, d2 = face_inverse(m1[0:128, :128] + r2[0:128, :], SECOND_RHO, NEAR_STEPS)
             up2[1].wait_recv()
             w0 = r2[128:192, :]
             gt2 = cat(m1[0:128, 128:256], m1[0:128, 256:] + cat(zero, w0).T, axis=1)
@@ -355,7 +384,7 @@
             st3[512:640, :] = f2x
             up3[3].start()
             up3[0].wait_recv()
-            k3, d3 = face_inverse(m2yy + r3[0:128, :])
+            k3, d3 = face_inverse(m2yy + r3[0:128, :], THIRD_RHO, NEAR_STEPS)
             up3[1].wait_recv()
             yx = r3[128:256, :]
             x3r = mm(k3, cat(m2yx, yx, axis=1) * d3)
@@ -386,6 +415,12 @@
             near_map = cat(x3r[:, :128], x2r[:, :128] - back[:, :128])
             far_map = cat(x3r[:, 128:], -back[:, 128:256])
             down_free = cat(b3, b2 - back[:, 256:])
+            up2[3].wait_recv()
+            outer_map = cat(r2[512:576, :], r2[448:512, :], axis=1)
+            outer_part = mm(outer_map, cat(near_map, far_map, down_free, axis=1))
+            near_map = cat(near_map, -outer_part[:, :128])
+            far_map = cat(far_map, -outer_part[:, 128:256])
+            down_free = cat(down_free, r2[576:640, :] - outer_part[:, 256:])
             up4[0].wait_recv()
             mix = r4[0:128, :]
             mix_t = mix.T
@@ -404,27 +439,28 @@
             u_far = mm(k5, (f3[128:] + r4[392:520, :] - mm(x4t, h4)) * d5)
             u_near = y4 - mm(x4, u_far)
             u_low = down_free - mm(near_map, y4) - mm(far_map, u_far)
-            dnst[0:128, :] = u_low[128:]
-            dnst[128:192, :] = u_low[64:128]
+            dnst[0:64, :] = u_low[256:]
             down2[0].start()
-            ur[0:128, :] = u_low[128:]
+            dnst[64:128, :] = u_low[192:256]
+            down2[1].start()
+            dnst[128:192, :] = u_low[128:192]
+            dnst[192:256, :] = u_low[64:128]
+            down2[2].start()
+            ur[0:128, :] = u_low[128:256]
             ur[128:256, :] = u_near
             ur[256:320, :] = u_low[:64]
-            for copy in up3 + up4 + down2:
+            ur[320:384, :] = zero
+            down1[0].start()
+            down1[1].start()
+            u_yi = x1b[...] - mm(x1r, ur[...])
+            uyi[...] = u_yi
+            down1[2].start()
+            uloc[0:64, :] = ur[0:64, :]
+            uloc[64:128, :] = ur[128:192, :]
+            uloc[128:192, :] = u_yi
+            uloc[192:256, :] = ur[256:320, :]
+            for copy in up3 + up4 + down2 + down1:
                 copy.wait_send()
-
-        ur[320:384, :] = zero
-        down1[0].start()
-        down1[1].start()
-        u_yi = x1b[...] - mm(x1r, ur[...])
-        uyi[...] = u_yi
-        down1[2].start()
-        uloc[0:64, :] = ur[0:64, :]
-        uloc[64:128, :] = ur[128:192, :]
-        uloc[128:192, :] = u_yi
-        uloc[192:256, :] = ur[256:320, :]
-        for copy in down1:
-            copy.wait_send()
 
     uloc[...] = uloc[...] + ut[...]
     u_b = cat(*[uloc[pl.ds(p, 64), :] for p in places])
@@ -450,7 +486,7 @@
         vmem = pl.BlockSpec(memory_space=pltpu.VMEM)
         anywhere = pl.BlockSpec(memory_space=pl.ANY)
         shapes = [(256, 256)] * 3 + [(1, 512), (512, 128), (256, 256), (256, 128), (256, 128), (2, 128, 128), (192, 256), (192, 128),
-                  (448, 128), (448, 128), (640, 128), (640, 128), (640, 128), (640, 128), (384, 128), (192, 128), (192, 128), (64, 128),
+                  (640, 128), (640, 128), (640, 128), (640, 128), (640, 128), (640, 128), (384, 128), (256, 128), (128, 128), (64, 128),
                   (192, 128), (256, 128), (64, 128)]
         dma = pltpu.SemaphoreType.DMA
         interior, boundary = pl.pallas_call(
@@ -458,7 +494,7 @@
             out_shape=(pltpu.VMEM((256, 128), F32), pltpu.VMEM((256, 128), F32)),
             in_specs=[anywhere] * 6,
             out_specs=(vmem, vmem),
-            scratch_shapes=[pltpu.VMEM(shape, F32) for shape in shapes] + [dma((6,)), dma((22,)), dma((22,)), dma((2, 4))],
+            scratch_shapes=[pltpu.VMEM(shape, F32) for shape in shapes] + [dma((6,)), dma((24,)), dma((24,)), dma((2, 4))],
             compiler_params=pltpu.CompilerParams(collective_id=0, has_side_effects=True),
         )(
             couple_inner.reshape(256, 256),

time: 31.8 us -> 30.7 us (0.965)
  Pallas kernels: 31.1 us -> 29.9 us
    pallas_call x1, Pallas kernels: 30.4 us -> 29.2 us  [local(): pl.pallas_call(kernel, out_shape=(pltpu.VMEM((256, 128), F32), pltpu.VMEM...]
where the time goes in v6:
time: 30.7 us; the launch traced here: 30.6 us
  Pallas kernels  29.9 us (97%)
  between operations  0.64 us (2%)
    pallas_call x1, Pallas kernels, local(): pl.pallas_call(kernel, out_shape=(pltpu.VMEM((256, 128), F32), pltpu.VMEM...  29.2 us
    pallas_call x1, Pallas kernels, local(): pl.pallas_call(store, out_shape=(jax.ShapeDtypeStruct((256, 128), F32),)...  0.72 us

profile of v6, /device:TPU:1, one launch (start us, length us, event | category | flops | bytes accessed | tf_op | source)
XLA Modules:
  0.0 30.6 jit_solution(1711925755353532204)
XLA Ops:
  0.6 29.2 %shard_map.77 = (f32[256,128]{1,0:T(8,128)S(1)}, f32[256,128]{1,0:T(8,128)S(1)}) custom-call(f32[256,256]{1,0:T(8,128)} %bitcast.7, f32[256,256]{1,0:T(8,128)} %bitcast.8, f32[256,256]{1,0:T(8,128)} %bitcast.9, f32[1,512]{1,0:T(1,128)} %bitcast.11, f32[512,128]{1,0:T(8,128)} %bitcast.10, f32[32,256]{1,0:T(8,128)} %top.1), custom_call_target="tpu_custom_call" | custom-call | tf_op jit(solution)/shard_map/pallas_call | solution.py:492
  29.9 0.7 %shard_map.78 = (f32[256,128]{1,0:T(8,128)}, f32[256,128]{1,0:T(8,128)}) custom-call(f32[256,128]{1,0:T(8,128)S(1)} %get-tuple-element.6.a, f32[256,128]{1,0:T(8,128)S(1)} %get-tuple-element.7.b), custom_call_target="tpu_custom_call" | custom-call | tf_op jit(solution)/shard_map/pallas_call | solution.py:507

commit v7 on v6

--- a/solution.py
+++ b/solution.py
@@ -60,8 +60,8 @@
         square = 2.0 * t * t
         alpha = square / (square - 1.0)
         if k == steps - 1:
-            s = alpha * (s + dot(s.astype(BF16), r.astype(BF16)))
-        elif k == steps - 2:
+            return s, r, alpha
+        if k == steps - 2:
             rs = split(r)
             p = mm_split(split(s), rs)
             r = alpha * dot(rs[0], rs[0]) - (alpha - 1.0) * eye
@@ -76,7 +76,14 @@
             r = alpha * p[:n] - (alpha - 1.0) * eye
             s = alpha * (s + p[n:])
         t = square - 1.0
-    return s
+
+
+def lift(r, x):
+    return x + dot(r.astype(BF16), x.astype(BF16))
+
+
+def closed(s, r, alpha):
+    return alpha * (s + dot(s.astype(BF16), r.astype(BF16)))
 
 
 def face_inverse(v, rho=FACE_RHO, steps=FACE_STEPS):
@@ -95,7 +102,7 @@
     return jnp.concatenate(parts, axis)
 
 
-def kernel(ci_h, cq_h, co_h, mg_h, src_h, top, out_in, out_b, ci, cq, co, mg, src, mloc, gloc, ut, tv, s1m, s1g, st2, r2, st3, r3, st4, r4, ur,
+def kernel(ci_h, cq_h, co_h, mg_h, src_h, top, out_in, out_b, ci, cq, co, mg, src, mloc, gloc, zq, ut, tv, s1m, s1g, st2, r2, st3, r3, st4, r4, ur,
            dnst, dn2, uyi, dn1, uloc, x1b, load, send, recv, tvrecv):
     loads = [pltpu.make_async_copy(h, v, load.at[k]) for k, (h, v) in enumerate(((ci_h, ci), (cq_h, cq), (mg_h, mg), (co_h, co), (src_h, src)))]
     for copy in loads:
@@ -143,10 +150,11 @@
     di = 1.0 / d_in
 
     di0 = di[:128]
-    s0 = inverse_of(inner[:128, :128] * di0, LEAF_RHO, LEAF_STEPS)
-    first = mm(s0, cat(inner[:128, 128:], q[:128], axis=1) * di0)
-    across, across_t = first[:, :128], inner[128:, :128]
-    second = mm(across_t, first)
+    open0 = inverse_of(inner[:128, :128] * di0, LEAF_RHO, LEAF_STEPS)
+    across_t = inner[128:, :128]
+    lifted0 = lift(open0[1], cat(inner[:128, 128:], q[:128], axis=1) * di0)
+    second = open0[2] * mm(mm(across_t, open0[0]), lifted0)
+    rest = q[128:] + second[:, 128:]
 
     pl.semaphore_wait(barrier, 15)
     on_x = 1 - lx // 2
@@ -176,14 +184,12 @@
     outer = jnp.where(on, 0.0, 0.5 * (o + o.T))
     d_out = (jnp.sum(outer, 1, keepdims=True) + jnp.sum(qt, 1, keepdims=True)) * (1.0 + m_out)
     e_out = jnp.where(on, d_out, -outer)
-    s1, di1 = face_inverse(jnp.where(on[:128, :128], d_in[128:], 0.0) - inner[128:, 128:] - second[:, :128], LEAF_RHO, LEAF_STEPS)
-
-    def leaf_solve(y0, rest):
-        z1 = mm(s1, rest * di1)
-        return cat(y0 + mm(across, z1), z1)
-
-    zq = leaf_solve(first[:, 128:], q[128:] + second[:, 128:])
-    m = e_out - mm(qt, zq)
+    first = open0[2] * mm(open0[0], lifted0)
+    across, y_q = first[:, :128], first[:, 128:]
+    e_out = e_out - mm(qt[:, :128], y_q)
+    open1, di1 = face_inverse(jnp.where(on[:128, :128], d_in[128:], 0.0) - inner[128:, 128:] - second[:, :128], LEAF_RHO, LEAF_STEPS)
+    lifted1 = lift(open1[1], rest * di1)
+    m = e_out - open1[2] * mm(mm(rest.T, open1[0]), lifted1)
     t0, t1 = m[:, :128], m[:, 128:]
     t0 = jnp.where(bx == 0, half_swap(t0), t0)
     t1 = jnp.where(by == 0, half_swap(t1), t1)
@@ -215,9 +221,14 @@
         up1[1].start()
 
     def leaf_flux():
+        s0, s1 = closed(*open0), closed(*open1)
+        z1 = open1[2] * mm(open1[0], lifted1)
+        zq[0:128, :] = y_q + mm(across, z1)
+        zq[128:256, :] = z1
         loads[4].wait()
         y0 = mm(s0, src[:128, :] * di0)
-        z = leaf_solve(y0, src[128:256, :] + mm(across_t, y0))
+        z1 = mm(s1, (src[128:256, :] + mm(across_t, y0)) * di1)
+        z = cat(y0 + mm(across, z1), z1)
         g = src[256:, :] + mm(qt, z)
         for k in range(4):
             gloc[pl.ds(places[k], 64), :] = g[64 * k : 64 * k + 64]
@@ -277,7 +288,7 @@
     def _():
         up1[0].wait_recv()
         v1 = mloc[128:192, 128:256] + s1m[128:192, 128:256]
-        k1, d1 = face_inverse(v1[:, :64], FIRST_RHO, NEAR_STEPS)
+        open_1, d1 = face_inverse(v1[:, :64], FIRST_RHO, NEAR_STEPS)
         up1[1].wait_recv()
 
         def left_of(x):
@@ -293,8 +304,9 @@
 
         gt1 = (wide_root(128) + wide_mate(128)) * d1
         g1 = cat(mloc[0:64, 128:256], s1m[0:64, 128:256], mloc[64:128, 128:256], s1m[64:128, 128:256], mloc[192:256, 128:256])[:, :64]
-        x1a = mm(k1, gt1[:, :128])
-        shared1 = cat(wide_root(0)[:, :128], wide_mate(0)[:, :128]) - mm(g1[:128], x1a)
+        half1 = open_1[2] * mm(g1, open_1[0])
+        lifted1a = lift(open_1[1], gt1[:, :128])
+        shared1 = cat(wide_root(0)[:, :128], wide_mate(0)[:, :128]) - mm(half1[:128], lifted1a)
         up2 = [
             remote(10, rows(st2, 0, 128), rows(r2, 0, 128), pair),
             remote(11, rows(st2, 128, 128), rows(r2, 128, 128), pair),
@@ -307,9 +319,11 @@
             st2[0:128, :] = shared1
             up2[0].start()
 
-        x1b_ = mm(k1, gt1[:, 128:])
-        x1r = cat(x1a, x1b_, axis=1)
-        p1l, p1r = mm(g1[128:], x1a), mm(g1, x1b_)
+        lifted1b = lift(open_1[1], gt1[:, 128:])
+        p1l, p1r = mm(half1[128:], lifted1a), mm(half1, lifted1b)
+        k1 = closed(*open_1)
+        x1a = mm(k1, gt1[:, :128])
+        x1r = cat(x1a, mm(k1, gt1[:, 128:]), axis=1)
         m1 = cat(
             cat(shared1, cat(wide_root(64)[:, :128], wide_mate(64)[:, :128], wide_root(192)[:, :128]) - p1l),
             cat(*[w[:, 128:] for w in (wide_root(0), wide_mate(0), wide_root(64), wide_mate(64), wide_root(192))]) - p1r,
@@ -350,11 +364,12 @@
         def _():
             f1 = flux1()
             up2[0].wait_recv()
-            k2, d2 = face_inverse(m1[0:128, :128] + r2[0:128, :], SECOND_RHO, NEAR_STEPS)
+            open_2, d2 = face_inverse(m1[0:128, :128] + r2[0:128, :], SECOND_RHO, NEAR_STEPS)
             up2[1].wait_recv()
             w0 = r2[128:192, :]
             gt2 = cat(m1[0:128, 128:256], m1[0:128, 256:] + cat(zero, w0).T, axis=1)
-            x2y = mm(k2, gt2[:, 128:] * d2)
+            gt2 = gt2 * d2
+            lifted2y = lift(open_2[1], gt2[:, 128:])
 
             up3 = [
                 remote(14, rows(st3, 0, 128), rows(r3, 0, 128), side_y),
@@ -364,14 +379,15 @@
             ]
             g2y = cat(m1[256:320, :128], w0)
             base2y = cat(m1[256:320, 128:], cat(zero, r2[192:256, :], axis=1))
-            m2yy = base2y[:, 128:] - mm(g2y, x2y)
+            half2y = open_2[2] * mm(g2y, open_2[0])
+            m2yy = base2y[:, 128:] - mm(half2y, lifted2y)
             st3[0:128, :] = m2yy
             up3[0].start()
-            x2x = mm(k2, gt2[:, :128] * d2)
-            x2r = cat(x2x, x2y, axis=1)
-            m2yx = base2y[:, :128] - mm(g2y, x2x)
+            m2yx = base2y[:, :128] - mm(half2y, lift(open_2[1], gt2[:, :128]))
             st3[128:256, :] = m2yx
             up3[1].start()
+            k2 = closed(*open_2)
+            x2r = mm(k2, gt2)
             g2x = m1[128:256, :128]
             m2x = m1[128:256, 128:] - mm(g2x, x2r)
             st3[256:384, :] = m2x[:, :128]
@@ -384,12 +400,12 @@
             st3[512:640, :] = f2x
             up3[3].start()
             up3[0].wait_recv()
-            k3, d3 = face_inverse(m2yy + r3[0:128, :], THIRD_RHO, NEAR_STEPS)
+            open_3, d3 = face_inverse(m2yy + r3[0:128, :], THIRD_RHO, NEAR_STEPS)
             up3[1].wait_recv()
             yx = r3[128:256, :]
-            x3r = mm(k3, cat(m2yx, yx, axis=1) * d3)
+            gt3 = cat(m2yx, yx, axis=1) * d3
             g3 = cat(m2x[:, 128:], yx.T)
-            p3 = mm(g3, x3r)
+            p3 = open_3[2] * mm(mm(g3, open_3[0]), lift(open_3[1], gt3))
 
             up4 = [
                 remote(18, rows(st4, 0, 136), rows(r4, 0, 136), side_x),
@@ -407,6 +423,8 @@
             up4[0].start()
             up4[1].start()
             up3[3].wait_recv()
+            k3 = closed(*open_3)
+            x3r = mm(k3, gt3)
             b3 = mm(k3, (f2y + r3[384:512, :]) * d3)
             f3 = cat(f2x, r3[512:640, :]) - mm(g3, b3)
             st4[264:520, :] = f3
@@ -424,13 +442,15 @@
             up4[0].wait_recv()
             mix = r4[0:128, :]
             mix_t = mix.T
-            k4, d4 = face_inverse(m00 + jnp.where(lower, mix, mix_t))
+            open_4, d4 = face_inverse(m00 + jnp.where(lower, mix, mix_t))
             up4[1].wait_recv()
             v01 = m01 + r4[136:264, :]
             v10 = v01.T
-            x4 = mm(k4, v01 * d4)
+            lifted4 = lift(open_4[1], v01 * d4)
             far_block = m11 + jnp.where(on128, jnp.broadcast_to(r4[128:129, :], (128, 128)), jnp.where(lower, mix_t, mix))
-            k5, d5 = face_inverse(far_block - mm(v10, x4))
+            open_5, d5 = face_inverse(far_block - open_4[2] * mm(mm(v10, open_4[0]), lifted4))
+            k4, k5 = closed(*open_4), closed(*open_5)
+            x4 = open_4[2] * mm(open_4[0], lifted4)
             x4t = x4.T
             far_map = far_map - mm(near_map, x4)
             up4[2].wait_recv()
@@ -465,7 +485,7 @@
     uloc[...] = uloc[...] + ut[...]
     u_b = cat(*[uloc[pl.ds(p, 64), :] for p in places])
     out_b[...] = u_b
-    out_in[...] = src[:256, :] + mm(zq, u_b)
+    out_in[...] = src[:256, :] + mm(zq[...], u_b)
     for away, copy, _ in top_sends:
 
         @pl.when(away)
@@ -485,7 +505,7 @@
     def local(couple_inner, couple_cross, couple_outer, margin, sources, top_values):
         vmem = pl.BlockSpec(memory_space=pltpu.VMEM)
         anywhere = pl.BlockSpec(memory_space=pl.ANY)
-        shapes = [(256, 256)] * 3 + [(1, 512), (512, 128), (256, 256), (256, 128), (256, 128), (2, 128, 128), (192, 256), (192, 128),
+        shapes = [(256, 256)] * 3 + [(1, 512), (512, 128), (256, 256), (256, 128), (256, 256), (256, 128), (2, 128, 128), (192, 256), (192, 128),
                   (640, 128), (640, 128), (640, 128), (640, 128), (640, 128), (640, 128), (384, 128), (256, 128), (128, 128), (64, 128),
                   (192, 128), (256, 128), (64, 128)]
         dma = pltpu.SemaphoreType.DMA

time: 30.7 us -> 29.9 us (0.974)
  Pallas kernels: 29.9 us -> 29.2 us
    pallas_call x1, Pallas kernels: 29.2 us -> 28.4 us  [local(): pl.pallas_call(kernel, out_shape=(pltpu.VMEM((256, 128), F32), pltpu.VMEM...]
where the time goes in v7:
time: 29.9 us; the launch traced here: 29.8 us
  Pallas kernels  29.2 us (98%)
  between operations  0.64 us (2%)
    pallas_call x1, Pallas kernels, local(): pl.pallas_call(kernel, out_shape=(pltpu.VMEM((256, 128), F32), pltpu.VMEM...  28.4 us
    pallas_call x1, Pallas kernels, local(): pl.pallas_call(store, out_shape=(jax.ShapeDtypeStruct((256, 128), F32),)...  0.72 us

profile of v7, /device:TPU:1, one launch (start us, length us, event | category | flops | bytes accessed | tf_op | source)
XLA Modules:
  0.0 29.8 jit_solution(8660609952803123926)
XLA Ops:
  0.6 28.4 %shard_map.77 = (f32[256,128]{1,0:T(8,128)S(1)}, f32[256,128]{1,0:T(8,128)S(1)}) custom-call(f32[256,256]{1,0:T(8,128)} %bitcast.7, f32[256,256]{1,0:T(8,128)} %bitcast.8, f32[256,256]{1,0:T(8,128)} %bitcast.9, f32[1,512]{1,0:T(1,128)} %bitcast.11, f32[512,128]{1,0:T(8,128)} %bitcast.10, f32[32,256]{1,0:T(8,128)} %top.1), custom_call_target="tpu_custom_call" | custom-call | tf_op jit(solution)/shard_map/pallas_call | solution.py:512
  29.1 0.7 %shard_map.78 = (f32[256,128]{1,0:T(8,128)}, f32[256,128]{1,0:T(8,128)}) custom-call(f32[256,128]{1,0:T(8,128)S(1)} %get-tuple-element.6.a, f32[256,128]{1,0:T(8,128)S(1)} %get-tuple-element.7.b), custom_call_target="tpu_custom_call" | custom-call | tf_op jit(solution)/shard_map/pallas_call | solution.py:527

commit v8 on v7

--- a/solution.py
+++ b/solution.py
@@ -102,8 +102,8 @@
     return jnp.concatenate(parts, axis)
 
 
-def kernel(ci_h, cq_h, co_h, mg_h, src_h, top, out_in, out_b, ci, cq, co, mg, src, mloc, gloc, zq, ut, tv, s1m, s1g, st2, r2, st3, r3, st4, r4, ur,
-           dnst, dn2, uyi, dn1, uloc, x1b, load, send, recv, tvrecv):
+def kernel(ci_h, cq_h, co_h, mg_h, src_h, top, out_in, out_b, ci, cq, co, mg, src, mloc, gloc, ut, tv, s1m, s1g, st2, r2, st3, r3, st4, r4, ur,
+           dnst, dn2, uyi, dn1, uloc, x1b, zq, zq_low, load, send, recv, tvrecv):
     loads = [pltpu.make_async_copy(h, v, load.at[k]) for k, (h, v) in enumerate(((ci_h, ci), (cq_h, cq), (mg_h, mg), (co_h, co), (src_h, src)))]
     for copy in loads:
         copy.start()
@@ -223,8 +223,7 @@
     def leaf_flux():
         s0, s1 = closed(*open0), closed(*open1)
         z1 = open1[2] * mm(open1[0], lifted1)
-        zq[0:128, :] = y_q + mm(across, z1)
-        zq[128:256, :] = z1
+        zq[...], zq_low[...] = split(cat(y_q + mm(across, z1), z1))
         loads[4].wait()
         y0 = mm(s0, src[:128, :] * di0)
         z1 = mm(s1, (src[128:256, :] + mm(across_t, y0)) * di1)
@@ -449,26 +448,31 @@
             lifted4 = lift(open_4[1], v01 * d4)
             far_block = m11 + jnp.where(on128, jnp.broadcast_to(r4[128:129, :], (128, 128)), jnp.where(lower, mix_t, mix))
             open_5, d5 = face_inverse(far_block - open_4[2] * mm(mm(v10, open_4[0]), lifted4))
-            k4, k5 = closed(*open_4), closed(*open_5)
+            k4 = closed(*open_4)
             x4 = open_4[2] * mm(open_4[0], lifted4)
             x4t = x4.T
             far_map = far_map - mm(near_map, x4)
             up4[2].wait_recv()
+            k5 = closed(*open_5)
             h4 = f3[:128] + r4[264:392, :]
             y4 = mm(k4, h4 * d4)
             u_far = mm(k5, (f3[128:] + r4[392:520, :] - mm(x4t, h4)) * d5)
-            u_near = y4 - mm(x4, u_far)
-            u_low = down_free - mm(near_map, y4) - mm(far_map, u_far)
-            dnst[0:64, :] = u_low[256:]
+            u_base = down_free - mm(near_map, y4)
+            last_far = split(u_far)
+            u_last = u_base[192:] - mm_split(split(far_map[192:]), last_far)
+            dnst[0:64, :] = u_last[64:]
+            dnst[64:128, :] = u_last[:64]
             down2[0].start()
-            dnst[64:128, :] = u_low[192:256]
             down2[1].start()
-            dnst[128:192, :] = u_low[128:192]
-            dnst[192:256, :] = u_low[64:128]
+            u_mid = u_base[64:192] - mm_split(split(far_map[64:192]), last_far)
+            dnst[128:192, :] = u_mid[64:]
+            dnst[192:256, :] = u_mid[:64]
             down2[2].start()
-            ur[0:128, :] = u_low[128:256]
-            ur[128:256, :] = u_near
-            ur[256:320, :] = u_low[:64]
+            u_own = cat(y4, u_base[:64]) - mm_split(split(cat(x4, far_map[:64])), last_far)
+            ur[0:64, :] = u_mid[64:]
+            ur[64:128, :] = u_last[:64]
+            ur[128:256, :] = u_own[:128]
+            ur[256:320, :] = u_own[128:]
             ur[320:384, :] = zero
             down1[0].start()
             down1[1].start()
@@ -485,7 +489,7 @@
     uloc[...] = uloc[...] + ut[...]
     u_b = cat(*[uloc[pl.ds(p, 64), :] for p in places])
     out_b[...] = u_b
-    out_in[...] = src[:256, :] + mm(zq[...], u_b)
+    out_in[...] = src[:256, :] + mm_split((zq[...], zq_low[...]), split(u_b))
     for away, copy, _ in top_sends:
 
         @pl.when(away)
@@ -505,7 +509,7 @@
     def local(couple_inner, couple_cross, couple_outer, margin, sources, top_values):
         vmem = pl.BlockSpec(memory_space=pltpu.VMEM)
         anywhere = pl.BlockSpec(memory_space=pl.ANY)
-        shapes = [(256, 256)] * 3 + [(1, 512), (512, 128), (256, 256), (256, 128), (256, 256), (256, 128), (2, 128, 128), (192, 256), (192, 128),
+        shapes = [(256, 256)] * 3 + [(1, 512), (512, 128), (256, 256), (256, 128), (256, 128), (2, 128, 128), (192, 256), (192, 128),
                   (640, 128), (640, 128), (640, 128), (640, 128), (640, 128), (640, 128), (384, 128), (256, 128), (128, 128), (64, 128),
                   (192, 128), (256, 128), (64, 128)]
         dma = pltpu.SemaphoreType.DMA
@@ -514,7 +518,7 @@
             out_shape=(pltpu.VMEM((256, 128), F32), pltpu.VMEM((256, 128), F32)),
             in_specs=[anywhere] * 6,
             out_specs=(vmem, vmem),
-            scratch_shapes=[pltpu.VMEM(shape, F32) for shape in shapes] + [dma((6,)), dma((24,)), dma((24,)), dma((2, 4))],
+            scratch_shapes=[pltpu.VMEM(shape, F32) for shape in shapes] + [pltpu.VMEM((256, 256), BF16)] * 2 + [dma((6,)), dma((24,)), dma((24,)), dma((2, 4))],
             compiler_params=pltpu.CompilerParams(collective_id=0, has_side_effects=True),
         )(
             couple_inner.reshape(256, 256),

time: 29.9 us -> 29.7 us (level)
  no operation moved by 1% of the time
where the time goes in v8:
time: 29.7 us; the launch traced here: 29.6 us
  Pallas kernels  29 us (98%)
  between operations  0.64 us (2%)
    pallas_call x1, Pallas kernels, local(): pl.pallas_call(kernel, out_shape=(pltpu.VMEM((256, 128), F32), pltpu.VMEM...  28.3 us
    pallas_call x1, Pallas kernels, local(): pl.pallas_call(store, out_shape=(jax.ShapeDtypeStruct((256, 128), F32),)...  0.72 us

profile of v8, /device:TPU:1, one launch (start us, length us, event | category | flops | bytes accessed | tf_op | source)
XLA Modules:
  0.0 29.6 jit_solution(18045716163645158902)
XLA Ops:
  0.6 28.3 %shard_map.77 = (f32[256,128]{1,0:T(8,128)S(1)}, f32[256,128]{1,0:T(8,128)S(1)}) custom-call(f32[256,256]{1,0:T(8,128)} %bitcast.7, f32[256,256]{1,0:T(8,128)} %bitcast.8, f32[256,256]{1,0:T(8,128)} %bitcast.9, f32[1,512]{1,0:T(1,128)} %bitcast.11, f32[512,128]{1,0:T(8,128)} %bitcast.10, f32[32,256]{1,0:T(8,128)} %top.1), custom_call_target="tpu_custom_call" | custom-call | tf_op jit(solution)/shard_map/pallas_call | solution.py:516
  28.9 0.7 %shard_map.78 = (f32[256,128]{1,0:T(8,128)}, f32[256,128]{1,0:T(8,128)}) custom-call(f32[256,128]{1,0:T(8,128)S(1)} %get-tuple-element.6.a, f32[256,128]{1,0:T(8,128)S(1)} %get-tuple-element.7.b), custom_call_target="tpu_custom_call" | custom-call | tf_op jit(solution)/shard_map/pallas_call | solution.py:531

commit v9 on v8

--- a/solution.py
+++ b/solution.py
@@ -156,6 +156,17 @@
     second = open0[2] * mm(mm(across_t, open0[0]), lifted0)
     rest = q[128:] + second[:, 128:]
 
+    qt = q.T
+    loads[3].wait()
+    o = co[...]
+    outer = jnp.where(on, 0.0, 0.5 * (o + o.T))
+    d_out = (jnp.sum(outer, 1, keepdims=True) + jnp.sum(qt, 1, keepdims=True)) * (1.0 + m_out)
+    e_out = jnp.where(on, d_out, -outer)
+    first = open0[2] * mm(open0[0], lifted0)
+    across, y_q = first[:, :128], first[:, 128:]
+    e_out = e_out - mm(qt[:, :128], y_q)
+    open1, di1 = face_inverse(jnp.where(on[:128, :128], d_in[128:], 0.0) - inner[128:, 128:] - second[:, :128], LEAF_RHO, LEAF_STEPS)
+    lifted1 = lift(open1[1], rest * di1)
     pl.semaphore_wait(barrier, 15)
     on_x = 1 - lx // 2
     top_sends = []
@@ -178,28 +189,22 @@
         def _():
             here.start()
 
-    qt = q.T
-    loads[3].wait()
-    o = co[...]
-    outer = jnp.where(on, 0.0, 0.5 * (o + o.T))
-    d_out = (jnp.sum(outer, 1, keepdims=True) + jnp.sum(qt, 1, keepdims=True)) * (1.0 + m_out)
-    e_out = jnp.where(on, d_out, -outer)
-    first = open0[2] * mm(open0[0], lifted0)
-    across, y_q = first[:, :128], first[:, 128:]
-    e_out = e_out - mm(qt[:, :128], y_q)
-    open1, di1 = face_inverse(jnp.where(on[:128, :128], d_in[128:], 0.0) - inner[128:, 128:] - second[:, :128], LEAF_RHO, LEAF_STEPS)
-    lifted1 = lift(open1[1], rest * di1)
-    m = e_out - open1[2] * mm(mm(rest.T, open1[0]), lifted1)
-    t0, t1 = m[:, :128], m[:, 128:]
-    t0 = jnp.where(bx == 0, half_swap(t0), t0)
-    t1 = jnp.where(by == 0, half_swap(t1), t1)
     places = [pl.multiple_of(p, 64) for p in (64 * (1 - bx), 64 * bx, 128 + 64 * (1 - by), 128 + 64 * by)]
-    for k in range(4):
-        mloc[pl.ds(places[k], 64), :] = cat(t0[64 * k : 64 * k + 64], t1[64 * k : 64 * k + 64], axis=1)
+    rest_t = open1[2] * rest.T
+    half_y = mm(rest_t[128:], open1[0])
+    m_yy = e_out[128:, 128:] - mm(half_y, lifted1[:, 128:])
+    m_yy = jnp.where(by == 0, half_swap(m_yy), m_yy)
+    for k in range(2):
+        mloc[pl.ds(places[2 + k], 64), 128:256] = m_yy[64 * k : 64 * k + 64]
+
+    def up1_block(k, row, height, column):
+        where = (pl.ds(row, height), pl.ds(column, 128))
+        return remote(k, mloc.at[where], s1m.at[where], mate)
 
     up1 = [
-        remote(4, rows(mloc, 128, 64), rows(s1m, 128, 64), mate),
-        remote(5, rows(mloc, 0, 128), rows(s1m, 0, 128), mate),
+        up1_block(4, 128, 64, 128),
+        up1_block(5, 0, 192, 0),
+        up1_block(24, 0, 128, 128),
         remote(6, rows(gloc, 0, 192), s1g, mate),
     ]
     down1 = [
@@ -218,7 +223,21 @@
     @pl.when(py == 0)
     def _():
         up1[0].start()
+
+    m_yx = e_out[128:, :128] - mm(half_y, lifted1[:, :128])
+    m_x = e_out[:128] - mm(mm(rest_t[:128], open1[0]), lifted1)
+    m_xx, m_xy = m_x[:, :128], m_x[:, 128:]
+    m_xx = jnp.where(bx == 0, half_swap(m_xx), m_xx)
+    m_yx = jnp.where(bx == 0, half_swap(m_yx), m_yx)
+    m_xy = jnp.where(by == 0, half_swap(m_xy), m_xy)
+    for k in range(2):
+        mloc[pl.ds(places[k], 64), :] = cat(m_xx[64 * k : 64 * k + 64], m_xy[64 * k : 64 * k + 64], axis=1)
+        mloc[pl.ds(places[2 + k], 64), 0:128] = m_yx[64 * k : 64 * k + 64]
+
+    @pl.when(py == 0)
+    def _():
         up1[1].start()
+        up1[2].start()
 
     def leaf_flux():
         s0, s1 = closed(*open0), closed(*open1)
@@ -263,7 +282,7 @@
     @pl.when(py == 0)
     def _():
         leaf_flux()
-        up1[2].start()
+        up1[3].start()
 
         @pl.when(px == 1)
         def _():
@@ -289,6 +308,7 @@
         v1 = mloc[128:192, 128:256] + s1m[128:192, 128:256]
         open_1, d1 = face_inverse(v1[:, :64], FIRST_RHO, NEAR_STEPS)
         up1[1].wait_recv()
+        up1[2].wait_recv()
 
         def left_of(x):
             return jnp.where(left, x, 0.0)
@@ -330,7 +350,7 @@
 
         def flux1():
             leaf_flux()
-            up1[2].wait_recv()
+            up1[3].wait_recv()
             b1 = mm(k1, (gloc[128:192, :] + s1g[128:192, :]) * d1)
             x1b[...] = b1
             return cat(gloc[0:64, :], s1g[0:64, :], gloc[64:128, :], s1g[64:128, :], gloc[192:256, :]) - mm(g1, b1)
@@ -385,12 +405,13 @@
             m2yx = base2y[:, :128] - mm(half2y, lift(open_2[1], gt2[:, :128]))
             st3[128:256, :] = m2yx
             up3[1].start()
+            g2x = m1[128:256, :128]
+            half2x = open_2[2] * mm(g2x, open_2[0])
+            m2x = m1[128:256, 128:] - mm(half2x, lift(open_2[1], gt2))
+            st3[256:384, :] = m2x[:, :128]
+            up3[2].start()
             k2 = closed(*open_2)
             x2r = mm(k2, gt2)
-            g2x = m1[128:256, :128]
-            m2x = m1[128:256, 128:] - mm(g2x, x2r)
-            st3[256:384, :] = m2x[:, :128]
-            up3[2].start()
             up2[2].wait_recv()
             b2 = mm(k2, (f1[0:128] + r2[256:384, :]) * d2)
             f2y = cat(f1[256:320], r2[384:448, :]) - mm(g2y, b2)
@@ -518,7 +539,7 @@
             out_shape=(pltpu.VMEM((256, 128), F32), pltpu.VMEM((256, 128), F32)),
             in_specs=[anywhere] * 6,
             out_specs=(vmem, vmem),
-            scratch_shapes=[pltpu.VMEM(shape, F32) for shape in shapes] + [pltpu.VMEM((256, 256), BF16)] * 2 + [dma((6,)), dma((24,)), dma((24,)), dma((2, 4))],
+            scratch_shapes=[pltpu.VMEM(shape, F32) for shape in shapes] + [pltpu.VMEM((256, 256), BF16)] * 2 + [dma((6,)), dma((25,)), dma((25,)), dma((2, 4))],
             compiler_params=pltpu.CompilerParams(collective_id=0, has_side_effects=True),
         )(
             couple_inner.reshape(256, 256),

time: 29.7 us -> 29.8 us (level)
  no operation moved by 1% of the time
where the time goes in v9:
time: 29.8 us; the launch traced here: 29.7 us
  Pallas kernels  29.1 us (98%)
  between operations  0.64 us (2%)
    pallas_call x1, Pallas kernels, local(): pl.pallas_call(kernel, out_shape=(pltpu.VMEM((256, 128), F32), pltpu.VMEM...  28.4 us
    pallas_call x1, Pallas kernels, local(): pl.pallas_call(store, out_shape=(jax.ShapeDtypeStruct((256, 128), F32),)...  0.72 us

profile of v9, /device:TPU:1, one launch (start us, length us, event | category | flops | bytes accessed | tf_op | source)
XLA Modules:
  0.0 29.7 jit_solution(4636807052566090489)
XLA Ops:
  0.6 28.4 %shard_map.77 = (f32[256,128]{1,0:T(8,128)S(1)}, f32[256,128]{1,0:T(8,128)S(1)}) custom-call(f32[256,256]{1,0:T(8,128)} %bitcast.7, f32[256,256]{1,0:T(8,128)} %bitcast.8, f32[256,256]{1,0:T(8,128)} %bitcast.9, f32[1,512]{1,0:T(1,128)} %bitcast.11, f32[512,128]{1,0:T(8,128)} %bitcast.10, f32[32,256]{1,0:T(8,128)} %top.1), custom_call_target="tpu_custom_call" | custom-call | tf_op jit(solution)/shard_map/pallas_call | solution.py:537
  29.0 0.7 %shard_map.78 = (f32[256,128]{1,0:T(8,128)}, f32[256,128]{1,0:T(8,128)}) custom-call(f32[256,128]{1,0:T(8,128)S(1)} %get-tuple-element.6.a, f32[256,128]{1,0:T(8,128)S(1)} %get-tuple-element.7.b), custom_call_target="tpu_custom_call" | custom-call | tf_op jit(solution)/shard_map/pallas_call | solution.py:552

commit v10 on v8

--- a/solution.py
+++ b/solution.py
@@ -156,6 +156,17 @@
     second = open0[2] * mm(mm(across_t, open0[0]), lifted0)
     rest = q[128:] + second[:, 128:]
 
+    qt = q.T
+    loads[3].wait()
+    o = co[...]
+    outer = jnp.where(on, 0.0, 0.5 * (o + o.T))
+    d_out = (jnp.sum(outer, 1, keepdims=True) + jnp.sum(qt, 1, keepdims=True)) * (1.0 + m_out)
+    e_out = jnp.where(on, d_out, -outer)
+    first = open0[2] * mm(open0[0], lifted0)
+    across, y_q = first[:, :128], first[:, 128:]
+    e_out = e_out - mm(qt[:, :128], y_q)
+    open1, di1 = face_inverse(jnp.where(on[:128, :128], d_in[128:], 0.0) - inner[128:, 128:] - second[:, :128], LEAF_RHO, LEAF_STEPS)
+    lifted1 = lift(open1[1], rest * di1)
     pl.semaphore_wait(barrier, 15)
     on_x = 1 - lx // 2
     top_sends = []
@@ -178,17 +189,6 @@
         def _():
             here.start()
 
-    qt = q.T
-    loads[3].wait()
-    o = co[...]
-    outer = jnp.where(on, 0.0, 0.5 * (o + o.T))
-    d_out = (jnp.sum(outer, 1, keepdims=True) + jnp.sum(qt, 1, keepdims=True)) * (1.0 + m_out)
-    e_out = jnp.where(on, d_out, -outer)
-    first = open0[2] * mm(open0[0], lifted0)
-    across, y_q = first[:, :128], first[:, 128:]
-    e_out = e_out - mm(qt[:, :128], y_q)
-    open1, di1 = face_inverse(jnp.where(on[:128, :128], d_in[128:], 0.0) - inner[128:, 128:] - second[:, :128], LEAF_RHO, LEAF_STEPS)
-    lifted1 = lift(open1[1], rest * di1)
     m = e_out - open1[2] * mm(mm(rest.T, open1[0]), lifted1)
     t0, t1 = m[:, :128], m[:, 128:]
     t0 = jnp.where(bx == 0, half_swap(t0), t0)

time: 29.7 us -> 29.8 us (level)
  no operation moved by 1% of the time
where the time goes in v10:
time: 29.8 us; the launch traced here: 29.7 us
  Pallas kernels  29 us (97%)
  between operations  0.64 us (2%)
    pallas_call x1, Pallas kernels, local(): pl.pallas_call(kernel, out_shape=(pltpu.VMEM((256, 128), F32), pltpu.VMEM...  28.3 us
    pallas_call x1, Pallas kernels, local(): pl.pallas_call(store, out_shape=(jax.ShapeDtypeStruct((256, 128), F32),)...  0.72 us

profile of v10, /device:TPU:1, one launch (start us, length us, event | category | flops | bytes accessed | tf_op | source)
XLA Modules:
  0.0 29.7 jit_solution(8942416714712206434)
XLA Ops:
  0.6 28.3 %shard_map.77 = (f32[256,128]{1,0:T(8,128)S(1)}, f32[256,128]{1,0:T(8,128)S(1)}) custom-call(f32[256,256]{1,0:T(8,128)} %bitcast.7, f32[256,256]{1,0:T(8,128)} %bitcast.8, f32[256,256]{1,0:T(8,128)} %bitcast.9, f32[1,512]{1,0:T(1,128)} %bitcast.11, f32[512,128]{1,0:T(8,128)} %bitcast.10, f32[32,256]{1,0:T(8,128)} %top.1), custom_call_target="tpu_custom_call" | custom-call | tf_op jit(solution)/shard_map/pallas_call | solution.py:516
  28.9 0.7 %shard_map.78 = (f32[256,128]{1,0:T(8,128)}, f32[256,128]{1,0:T(8,128)}) custom-call(f32[256,128]{1,0:T(8,128)S(1)} %get-tuple-element.6.a, f32[256,128]{1,0:T(8,128)S(1)} %get-tuple-element.7.b), custom_call_target="tpu_custom_call" | custom-call | tf_op jit(solution)/shard_map/pallas_call | solution.py:531
